TPU v7x, 128 devices: a whole 4x4x4 slice. The times are simulated.
128 devices in a mesh: dp: 16 (over y, z), mp: 8 (over x, core).
Axes of the slice: x: 4, y: 4, z: 4, core: 2. Of those that a mesh axis runs over, the one named last changes fastest.
Arguments:
- grad_out: bfloat16 [16384, 6144], P(('dp', 'mp')), may hold values from -40 to 40
- context: bfloat16 [16384, 6144], P('dp', 'mp'), may hold values from -47 to 47
- weight: bfloat16 [6144, 6144], P(None, 'mp'), may hold values from -0.078125 to 0.078125
- master: float32 [6144, 6144], P('dp', 'mp'), may hold values from -0.6 to 0.6
- moment_q: bfloat16 [6144, 6144], P('dp', 'mp'), may hold values from -440 to 440
- second_moment: float32 [6144, 6144], P('dp', 'mp'), may hold values from 0.02 to 1
- moment_scale: float32 [], replicated, may hold values from 300 to 900
- scale_boost: float32 [], replicated, may hold values from 1.25 to 2
Outputs:
- input_grad: bfloat16 [16384, 6144], P('dp', 'mp')
- new_master: float32 [6144, 6144], P('dp', 'mp')
- new_moment_q: bfloat16 [6144, 6144], P('dp', 'mp')
- new_second: float32 [6144, 6144], P('dp', 'mp')
- new_scale: float32 [], replicated
- grad_scale: float32 [], replicated
- new_weight: bfloat16 [6144, 6144], P(None, 'mp')
All inputs are finite; a program needn't handle non-finite values. Where the computation divides by a largest or mean magnitude, that divisor is 1e-20 or more.
Results may differ from a plain program's by a relative error of at most 0.014.
Values may be sent and summed in bfloat16 or wider, within the bound.
No kernel may reach another device: no remote copies, remote signals or barrier semaphores. Data moves between devices by JAX's collectives and lax.ppermute only.
A program may use at most 128 MiB of HBM per device.

v0:
```python
import math

import jax
import jax.numpy as jnp
from jax import lax
from jax.sharding import PartitionSpec as P

D = 6144
HD = 6144


quant_top = 448.0
peak_eps = 1e-06
norm_eps = 1e-06
clip_rms = 0.5
beta_one = 0.9
beta_two = 0.95
bias_one = 1.0 - 0.9**10
bias_two = 1.0 - 0.95**10
adam_eps = 1e-08
rate_value = 0.01
decay_value = 0.1
contract_rows = (((0,), (0,)), ((), ()))


def input_product(full_grad, weight):
    return jnp.dot(full_grad, weight, preferred_element_type=jnp.float32).astype(jnp.bfloat16)


def weight_gradient(full_grad, context, scale_boost):
    held = lax.dot_general(full_grad, context, contract_rows, preferred_element_type=jnp.float32)
    local_peak = jnp.max(jnp.abs(held))
    peak = lax.pmax(local_peak, ("dp", "mp"))
    grad_scale = quant_top * scale_boost / (peak + peak_eps)
    scaled = held * grad_scale
    summed = lax.psum_scatter(
        jnp.clip(scaled, -quant_top, quant_top).astype(jnp.bfloat16),
        "dp",
        scatter_dimension=0,
        tiled=True,
    ).astype(jnp.float32)
    return (summed, grad_scale)


def local(grad_out, context, weight, master, moment_q, second_moment, moment_scale, scale_boost):
    full_grad = lax.all_gather(grad_out, "mp", axis=0, tiled=True)
    input_grad = input_product(full_grad, weight)
    summed, grad_scale = weight_gradient(full_grad, context, scale_boost)
    gradient = summed / grad_scale
    squares = lax.psum(jnp.sum(gradient * gradient), ("dp", "mp"))
    norm_value = jnp.sqrt(squares + norm_eps)
    clip_factor = clip_rms * math.sqrt(D * HD) / norm_value
    step_grad = clip_factor * gradient
    old_moment = moment_q.astype(jnp.float32) / moment_scale
    moment = beta_one * old_moment + (1.0 - beta_one) * step_grad
    new_second = beta_two * second_moment + (1.0 - beta_two) * step_grad * step_grad
    update = moment / bias_one / (jnp.sqrt(new_second / bias_two) + adam_eps) + decay_value * master
    new_master = master - rate_value * update
    moment_top = lax.pmax(jnp.max(jnp.abs(moment)), ("dp", "mp"))
    new_scale = quant_top / (moment_top + peak_eps)
    new_moment_q = (moment * new_scale).astype(jnp.bfloat16)
    new_weight = lax.all_gather(new_master.astype(jnp.bfloat16), "dp", axis=0, tiled=True)
    return (input_grad, new_master, new_moment_q, new_second, new_scale, grad_scale, new_weight)


def solution(mesh):
    return jax.shard_map(
        local,
        mesh=mesh,
        in_specs=(
            P(("dp", "mp"), None),
            P("dp", "mp"),
            P(None, "mp"),
            P("dp", "mp"),
            P("dp", "mp"),
            P("dp", "mp"),
            P(),
            P(),
        ),
        out_specs=(
            P("dp", "mp"),
            P("dp", "mp"),
            P("dp", "mp"),
            P("dp", "mp"),
            P(),
            P(),
            P(None, "mp"),
        ),
        check_vma=False,
    )
```

profile of v0, /device:TPU:1, one launch (start us, length us, event | category | flops | bytes accessed | tf_op | source)
XLA Modules:
  0.0 430.7 jit_solution(13931755045824228183)
XLA Ops:
  7.2 0.0 copy-start
  7.2 0.0 all-gather.3.cloned.1.call-start
  7.2 0.7 all-gather.3.cloned.1.call-update
  7.9 0.0 reduce-scatter.2.cloned.1.call-start
  8.6 72.1 %all-gather.3.cloned.1.call-done = bf16[1024,6144]{1,0:T(8,128)(2,1)} async-done(((bf16[128,6144]{1,0:T(8,128)(2,1)}), bf16[1024,6144]{1,0:T(8,128)(2,1)}) %all-gather.3.cloned.1.call-update) | async-done | bytes 12582928 | tf_op jit(solution)/shard_map/all_gather | solution.py:46
  80.7 0.0 copy-done
  80.7 17.7 %abs_reduce_fusion = (f32[]{:T(128)}, f32[6144,768]{1,0:T(8,128)}) fusion(bf16[1024,6144]{1,0:T(8,128)(2,1)} %all-gather.3.cloned.1.call-done, bf16[1024,768]{1,0:T(8,128)(2,1)S(1)} %copy-done), kind=kOutput, calls=%fused_computation.1 | convolution fusion | flops 9673113600 | bytes 33030148 | tf_op jit(solution)/shard_map/dot_general | solution.py:31
  98.3 64.9 %pmax.14 = f32[]{:T(128)} all-reduce(f32[]{:T(128)} %get-tuple-element.11), channel_id=1, replica_groups=mesh['dp'=16,'mp'=8] {'dp','mp'}, use_global_device_ids=true, to_apply=%region_1.0 | all-reduce | flops 1 | bytes 8 | tf_op jit(solution)/shard_map/pmax | solution.py:33
  164.0 11.6 %clamp_convert_fusion = bf16[6144,768]{1,0:T(8,128)(2,1)} fusion(f32[6144,768]{1,0:T(8,128)} %get-tuple-element.12, f32[]{:T(128)} %div.38), kind=kLoop, calls=%fused_computation | loop fusion | flops 14155776 | bytes 28311556 | tf_op jit(solution)/shard_map/convert_element_type | solution.py:37
  175.5 0.0 copy-start.2
  175.5 0.0 copy-start.3
  175.5 0.0 reduce-scatter.2.cloned.1.call-update
  175.5 0.0 all-gather.5.cloned.1.call-start
  175.6 83.8 %reduce-scatter.2.cloned.1.call-done = bf16[384,768]{1,0:T(8,128)(2,1)} async-done(((bf16[6144,768]{1,0:T(8,128)(2,1)}), bf16[384,768]{1,0:T(8,128)(2,1)}) %reduce-scatter.2.cloned.1.call-update) | async-done | bytes 589840 | tf_op jit(solution)/shard_map/reduce_scatter | solution.py:36
  259.4 2.0 multiply_reduce_fusion
  262.0 65.6 %psum.7 = f32[]{:T(128)} all-reduce(f32[]{:T(128)} %multiply_reduce_fusion), channel_id=1, replica_groups=mesh['dp'=16,'mp'=8] {'dp','mp'}, use_global_device_ids=true, to_apply=%region_4.5 | all-reduce | flops 1 | bytes 8 | tf_op jit(solution)/shard_map/psum | solution.py:50
  328.3 0.0 copy-done.2
  328.3 0.0 copy-done.3
  328.3 4.1 fusion.1
  332.4 0.0 all-gather.5.cloned.1.call-update
  332.5 0.7 abs_reduce_fusion.1
  333.1 15.6 %convolution_convert_fusion = bf16[1024,768]{1,0:T(8,128)(2,1)} fusion(bf16[1024,6144]{1,0:T(8,128)(2,1)} %all-gather.3.cloned.1.call-done, bf16[6144,768]{1,0:T(8,128)(2,1)} %param.10), kind=kOutput, calls=%fused_computation.3 | convolution fusion | flops 9664462848 | bytes 23592960 | tf_op jit(solution)/shard_map/dot_general | solution.py:27
  348.8 63.4 %pmax.15 = f32[]{:T(128)} all-reduce(f32[]{:T(128)} %abs_reduce_fusion.1), channel_id=1, replica_groups=mesh['dp'=16,'mp'=8] {'dp','mp'}, use_global_device_ids=true, to_apply=%region_6.7 | all-reduce | flops 1 | bytes 8 | tf_op jit(solution)/shard_map/pmax | solution.py:59
  412.9 0.9 multiply_convert_fusion
  413.8 0.0 all-gather.5.cloned.1.call-done
  413.8 0.0 copy-start.1
  413.8 8.1 %copy.18 = bf16[6144,768]{1,0:T(8,128)(2,1)} copy(bf16[6144,768]{1,0:T(8,128)(2,1)} %all-gather.5.cloned.1.call-done) | data formatting | bytes 18874368
  421.9 0.0 copy-done.1
Async XLA Ops:
  7.2 73.5 %copy-start = (bf16[1024,768]{1,0:T(8,128)(2,1)S(1)}, bf16[1024,768]{1,0:T(8,128)(2,1)}, u32[]{:S(2)}) copy-start(bf16[1024,768]{1,0:T(8,128)(2,1)} %param.9) | copy-start | bytes 4718596
  7.2 73.5 %all-gather.3.cloned.1.call-start = ((), (), s32[]{:S(2)}) async-start(), calls=%async_computation.1 | async-start | bytes 14155776 | tf_op jit(solution)/shard_map/all_gather | solution.py:46
  7.9 251.5 %reduce-scatter.2.cloned.1.call-start = ((), (), s32[]{:S(2)}) async-start(), calls=%async_computation.2 | async-start | bytes 10027008 | tf_op jit(solution)/shard_map/reduce_scatter | solution.py:36
  175.5 152.8 %copy-start.2 = (f32[384,768]{1,0:T(8,128)S(1)}, f32[384,768]{1,0:T(8,128)}, u32[]{:S(2)}) copy-start(f32[384,768]{1,0:T(8,128)} %param.11) | copy-start | bytes 3538948
  175.5 152.8 %copy-start.3 = (bf16[384,768]{1,0:T(8,128)(2,1)S(1)}, bf16[384,768]{1,0:T(8,128)(2,1)}, u32[]{:S(2)}) copy-start(bf16[384,768]{1,0:T(8,128)(2,1)} %param.12) | copy-start | bytes 1769476
  175.5 238.2 %all-gather.5.cloned.1.call-start = ((), (), s32[]{:S(2)}) async-start(), calls=%async_computation.3 | async-start | bytes 10027008 | tf_op jit(solution)/shard_map/all_gather | solution.py:62
  413.8 8.2 %copy-start.1 = (bf16[1024,768]{1,0:T(8,128)(2,1)S(1)}, bf16[1024,768]{1,0:T(8,128)(2,1)}, u32[]{:S(2)}) copy-start(bf16[1024,768]{1,0:T(8,128)(2,1)} %param.9) | copy-start | bytes 4718596
Sparse Core Ops, SparseCore 0:
  9.7 70.9 all-gather.2
  175.7 83.6 reduce-scatter.1
  332.6 72.7 all-gather.4
where the time goes:
time: 431 us
  blocking collectives  194 us (45%)
  waiting for transfers between devices  157 us (36%)
  matrix products  33.3 us (8%)
  between operations  19.4 us (5%)
  other arithmetic  19.2 us (4%)
  local copies, waits for them, and re-layouts  8.17 us (2%)
    reduce_scatter x1, waiting for transfers between devices, weight_gradient(): lax.psum_scatter(jnp.clip(scaled, -quant_top, quant_top).astype(jnp.bfloa...  83.8 us
    all_gather x1, waiting for transfers between devices, local(): full_grad = lax.all_gather(grad_out, 'mp', axis=0, tiled=True)  72.1 us
    psum x1, blocking collectives, local(): squares = lax.psum(jnp.sum(gradient * gradient), ('dp', 'mp'))  65.6 us
    pmax x1, blocking collectives, weight_gradient(): peak = lax.pmax(local_peak, ('dp', 'mp'))  64.9 us
    pmax x1, blocking collectives, local(): moment_top = lax.pmax(jnp.max(jnp.abs(moment)), ('dp', 'mp'))  63.4 us
    dot_general x1, matrix products, weight_gradient(): lax.dot_general(full_grad, context, contract_rows, preferred_element_type...  17.7 us
    dot_general x1, matrix products, input_product(): jnp.dot(full_grad, weight, preferred_element_type=jnp.float32)  15.6 us
    convert_element_type x1, other arithmetic, weight_gradient(): jnp.clip(scaled, -quant_top, quant_top).astype(jnp.bfloat16)  11.6 us
  transfers between devices with their start and end apart: 3, of which 2 were waited for; matrix products, arithmetic and copies ran while one was open for 4% of the time, Pallas kernels for 0%

commit v1 on v0

--- a/solution.py
+++ b/solution.py
@@ -7,6 +7,8 @@
 
 D = 6144
 HD = 6144
+N_DEV = 128
+LANES = 128
 
 
 quant_top = 448.0
@@ -27,10 +29,23 @@
     return jnp.dot(full_grad, weight, preferred_element_type=jnp.float32).astype(jnp.bfloat16)
 
 
+def spread(value):
+    rows = jnp.broadcast_to(value, (N_DEV, LANES))
+    return lax.all_to_all(rows, ("dp", "mp"), 0, 0, tiled=True)
+
+
+def global_max(value):
+    return jnp.max(spread(value))
+
+
+def global_sum(value):
+    return jnp.sum(spread(value)[:, 0])
+
+
 def weight_gradient(full_grad, context, scale_boost):
     held = lax.dot_general(full_grad, context, contract_rows, preferred_element_type=jnp.float32)
     local_peak = jnp.max(jnp.abs(held))
-    peak = lax.pmax(local_peak, ("dp", "mp"))
+    peak = global_max(local_peak)
     grad_scale = quant_top * scale_boost / (peak + peak_eps)
     scaled = held * grad_scale
     summed = lax.psum_scatter(
@@ -47,7 +62,7 @@
     input_grad = input_product(full_grad, weight)
     summed, grad_scale = weight_gradient(full_grad, context, scale_boost)
     gradient = summed / grad_scale
-    squares = lax.psum(jnp.sum(gradient * gradient), ("dp", "mp"))
+    squares = global_sum(jnp.sum(gradient * gradient))
     norm_value = jnp.sqrt(squares + norm_eps)
     clip_factor = clip_rms * math.sqrt(D * HD) / norm_value
     step_grad = clip_factor * gradient
@@ -56,7 +71,7 @@
     new_second = beta_two * second_moment + (1.0 - beta_two) * step_grad * step_grad
     update = moment / bias_one / (jnp.sqrt(new_second / bias_two) + adam_eps) + decay_value * master
     new_master = master - rate_value * update
-    moment_top = lax.pmax(jnp.max(jnp.abs(moment)), ("dp", "mp"))
+    moment_top = global_max(jnp.max(jnp.abs(moment)))
     new_scale = quant_top / (moment_top + peak_eps)
     new_moment_q = (moment * new_scale).astype(jnp.bfloat16)
     new_weight = lax.all_gather(new_master.astype(jnp.bfloat16), "dp", axis=0, tiled=True)

time: 431 us -> 330 us (0.77)
  blocking collectives: 194 us -> 0 us
  waiting for transfers between devices: 157 us -> 222 us
  starting transfers between devices: 0.12 us -> 21.3 us
    pmax x2 -> x0, blocking collectives: 128 us -> none  [the longest x1 64.9 us: weight_gradient(): peak = lax.pmax(local_peak, ('dp', 'mp'))]
    psum x1 -> x0, blocking collectives: 65.6 us -> none  [local(): squares = lax.psum(jnp.sum(gradient * gradient), ('dp', 'mp'))]
    all_gather x1, waiting for transfers between devices: 0.01 us -> 48 us  [local(): lax.all_gather(new_master.astype(jnp.bfloat16), 'dp', axis=0, tiled=True)]
    all_to_all x0 -> x3, starting transfers between devices: none -> 21.1 us  [spread(): return lax.all_to_all(rows, ('dp', 'mp'), 0, 0, tiled=True)]
    all_to_all x0 -> x3, waiting for transfers between devices: none -> 17.5 us  [spread(): return lax.all_to_all(rows, ('dp', 'mp'), 0, 0, tiled=True)]
  transfers between devices with their start and end apart: 3 -> 6, of which waited for: 2 -> 5; matrix products, arithmetic and copies ran while one was open for 4% -> 6% of each run, Pallas kernels for 0% -> 0%
where the time goes in v1:
time: 330 us
  waiting for transfers between devices  222 us (67%)
  matrix products  33.5 us (10%)
  starting transfers between devices  21.3 us (6%)
  other arithmetic  21.1 us (6%)
  between operations  19.4 us (6%)
  local copies, waits for them, and re-layouts  12.1 us (4%)
    reduce_scatter x1, waiting for transfers between devices, weight_gradient(): lax.psum_scatter(jnp.clip(scaled, -quant_top, quant_top).astype(jnp.bfloa...  83.3 us
    all_gather x1, waiting for transfers between devices, local(): full_grad = lax.all_gather(grad_out, 'mp', axis=0, tiled=True)  72.8 us
    all_gather x1, waiting for transfers between devices, local(): lax.all_gather(new_master.astype(jnp.bfloat16), 'dp', axis=0, tiled=True)  48 us
    all_to_all x3, starting transfers between devices, spread(): return lax.all_to_all(rows, ('dp', 'mp'), 0, 0, tiled=True)  21.1 us
    dot_general x1, matrix products, weight_gradient(): lax.dot_general(full_grad, context, contract_rows, preferred_element_type...  17.7 us
    all_to_all x3, waiting for transfers between devices, spread(): return lax.all_to_all(rows, ('dp', 'mp'), 0, 0, tiled=True)  17.5 us
    dot_general x1, matrix products, input_product(): jnp.dot(full_grad, weight, preferred_element_type=jnp.float32)  15.8 us
    convert_element_type x1, other arithmetic, weight_gradient(): jnp.clip(scaled, -quant_top, quant_top).astype(jnp.bfloat16)  11.6 us
  transfers between devices with their start and end apart: 6, of which 5 were waited for; matrix products, arithmetic and copies ran while one was open for 6% of the time, Pallas kernels for 0%

profile of v1, /device:TPU:1, one launch (start us, length us, event | category | flops | bytes accessed | tf_op | source)
XLA Modules:
  0.0 329.5 jit_solution(7558855803893621168)
XLA Ops:
  7.2 0.0 copy-start
  7.2 0.0 all-gather.3.cloned.1.call-start
  7.2 0.7 all-gather.3.cloned.1.call-update
  7.9 72.8 %all-gather.3.cloned.1.call-done = bf16[1024,6144]{1,0:T(8,128)(2,1)} async-done(((bf16[128,6144]{1,0:T(8,128)(2,1)}), bf16[1024,6144]{1,0:T(8,128)(2,1)}) %all-gather.3.cloned.1.call-update) | async-done | bytes 12582928 | tf_op jit(solution)/shard_map/all_gather | solution.py:61
  80.7 0.0 copy-done
  80.7 17.7 %abs_reduce_fusion = (f32[]{:T(128)}, f32[6144,768]{1,0:T(8,128)}) fusion(bf16[1024,6144]{1,0:T(8,128)(2,1)} %all-gather.3.cloned.1.call-done, bf16[1024,768]{1,0:T(8,128)(2,1)S(1)} %copy-done), kind=kOutput, calls=%fused_computation.1 | convolution fusion | flops 9673113600 | bytes 33030148 | tf_op jit(solution)/shard_map/dot_general | solution.py:46
  98.3 1.3 broadcast_in_dim.9
  99.6 8.3 %all-to-all-start = ((f32[128,1,128]{2,1,0:T(1,128)}), f32[128,1,128]{2,1,0:T(1,128)S(1)}, u32[]{:S(2)}, u32[]{:S(2)}) async-start(f32[128,1,128]{2,1,0:T(1,128)} %broadcast_in_dim.9), calls=%async_computation | async-start | bytes 131072 | tf_op jit(solution)/shard_map/all_to_all | solution.py:34
  107.9 0.0 reduce-scatter.2.cloned.1.call-start
  108.6 8.7 %all-to-all-done = f32[128,1,128]{2,1,0:T(1,128)S(1)} async-done(((f32[128,1,128]{2,1,0:T(1,128)}), f32[128,1,128]{2,1,0:T(1,128)S(1)}, u32[]{:S(2)}, u32[]{:S(2)}) %all-to-all-start) | async-done | bytes 65568 | tf_op jit(solution)/shard_map/all_to_all | solution.py:34
  117.3 0.6 reduce_max.37
  118.6 11.6 %clamp_convert_fusion = bf16[6144,768]{1,0:T(8,128)(2,1)} fusion(f32[6144,768]{1,0:T(8,128)} %get-tuple-element.12, f32[]{:T(128)} %div.38), kind=kLoop, calls=%fused_computation | loop fusion | flops 14155776 | bytes 28311556 | tf_op jit(solution)/shard_map/convert_element_type | solution.py:52
  130.2 0.0 reduce-scatter.2.cloned.1.call-update
  130.2 83.3 %reduce-scatter.2.cloned.1.call-done = bf16[384,768]{1,0:T(8,128)(2,1)} async-done(((bf16[6144,768]{1,0:T(8,128)(2,1)}), bf16[384,768]{1,0:T(8,128)(2,1)}) %reduce-scatter.2.cloned.1.call-update) | async-done | bytes 589840 | tf_op jit(solution)/shard_map/reduce_scatter | solution.py:51
  213.5 2.0 multiply_reduce_fusion
  215.5 1.3 broadcast_in_dim.10
  216.8 8.3 %all-to-all-start.1 = ((f32[128,1,128]{2,1,0:T(1,128)}), f32[128,1,128]{2,1,0:T(1,128)S(1)}, u32[]{:S(2)}, u32[]{:S(2)}) async-start(f32[128,1,128]{2,1,0:T(1,128)} %broadcast_in_dim.10), calls=%async_computation.2 | async-start | bytes 131072 | tf_op jit(solution)/shard_map/all_to_all | solution.py:34
  225.1 0.0 all-gather.5.cloned.1.call-start
  225.8 8.7 %all-to-all-done.1 = f32[128,1,128]{2,1,0:T(1,128)S(1)} async-done(((f32[128,1,128]{2,1,0:T(1,128)}), f32[128,1,128]{2,1,0:T(1,128)S(1)}, u32[]{:S(2)}, u32[]{:S(2)}) %all-to-all-start.1) | async-done | bytes 65568 | tf_op jit(solution)/shard_map/all_to_all | solution.py:34
  234.5 0.6 slice_reduce_fusion
  235.9 0.0 copy-done.3
  235.9 4.1 %fusion.1 = (bf16[384,768]{1,0:T(8,128)(2,1)}, f32[384,768]{1,0:T(8,128)}, f32[384,768]{1,0:T(8,128)S(1)}, f32[384,768]{1,0:T(8,128)}) fusion(f32[384,768]{1,0:T(8,128)S(1)} %copy-done.3, f32[]{:T(128)} %div.38, bf16[384,768]{1,0:T(8,128)(2,1)S(1)} %copy-done.2, f32[]{:T(128)S(6)} %div.41, f32[]{:T(128)S(6)} %copy.20, bf16[384,768]{1,0:T(8,128)(2,1)} %param.12, ...), kind=kLoop, calls=%fused_computation.12 | loop fusion | flops 6193152 | bytes 7667724 | tf_op jit(solution)/shard_map/convert_element_type | solution.py:77
  240.0 0.0 all-gather.5.cloned.1.call-update
  240.0 0.7 abs_reduce_fusion.1
  240.7 1.3 broadcast_in_dim.11
  242.0 4.6 %all-to-all-start.2 = ((f32[128,1,128]{2,1,0:T(1,128)}), f32[128,1,128]{2,1,0:T(1,128)S(1)}, u32[]{:S(2)}, u32[]{:S(2)}) async-start(f32[128,1,128]{2,1,0:T(1,128)} %broadcast_in_dim.11), calls=%async_computation.3 | async-start | bytes 131072 | tf_op jit(solution)/shard_map/all_to_all | solution.py:34
  246.6 15.8 %convolution_convert_fusion = bf16[1024,768]{1,0:T(8,128)(2,1)} fusion(bf16[1024,6144]{1,0:T(8,128)(2,1)} %all-gather.3.cloned.1.call-done, bf16[6144,768]{1,0:T(8,128)(2,1)} %param.10), kind=kOutput, calls=%fused_computation.3 | convolution fusion | flops 9664462848 | bytes 23592960 | tf_op jit(solution)/shard_map/dot_general | solution.py:29
  262.5 0.0 all-to-all-done.2
  262.5 0.6 reduce_max.39
  263.8 0.9 multiply_convert_fusion
  264.7 48.0 %all-gather.5.cloned.1.call-done = bf16[6144,768]{1,0:T(8,128)(2,1)} async-done(((bf16[384,768]{1,0:T(8,128)(2,1)}), bf16[6144,768]{1,0:T(8,128)(2,1)}) %all-gather.5.cloned.1.call-update) | async-done | bytes 9437200 | tf_op jit(solution)/shard_map/all_gather | solution.py:77
  312.6 8.1 %copy.22 = bf16[6144,768]{1,0:T(8,128)(2,1)} copy(bf16[6144,768]{1,0:T(8,128)(2,1)} %all-gather.5.cloned.1.call-done) | data formatting | bytes 18874368
  (5 shorter events, 0.0 us)
Async XLA Ops:
  7.2 73.5 %copy-start = (bf16[1024,768]{1,0:T(8,128)(2,1)S(1)}, bf16[1024,768]{1,0:T(8,128)(2,1)}, u32[]{:S(2)}) copy-start(bf16[1024,768]{1,0:T(8,128)(2,1)} %param.9) | copy-start | bytes 4718596
  7.2 73.5 %all-gather.3.cloned.1.call-start = ((), (), s32[]{:S(2)}) async-start(), calls=%async_computation.4 | async-start | bytes 14155776 | tf_op jit(solution)/shard_map/all_gather | solution.py:61
  99.6 17.7 %all-to-all-start = ((f32[128,1,128]{2,1,0:T(1,128)}), f32[128,1,128]{2,1,0:T(1,128)S(1)}, u32[]{:S(2)}, u32[]{:S(2)}) async-start(f32[128,1,128]{2,1,0:T(1,128)} %broadcast_in_dim.9), calls=%async_computation | async-start | bytes 131072 | tf_op jit(solution)/shard_map/all_to_all | solution.py:34
  107.9 105.6 %reduce-scatter.2.cloned.1.call-start = ((), (), s32[]{:S(2)}) async-start(), calls=%async_computation.5 | async-start | bytes 10027008 | tf_op jit(solution)/shard_map/reduce_scatter | solution.py:51
  130.2 105.7 %copy-start.3 = (f32[384,768]{1,0:T(8,128)S(1)}, f32[384,768]{1,0:T(8,128)}, u32[]{:S(2)}) copy-start(f32[384,768]{1,0:T(8,128)} %param.11) | copy-start | bytes 3538948
  213.5 22.4 %copy-start.2 = (bf16[384,768]{1,0:T(8,128)(2,1)S(1)}, bf16[384,768]{1,0:T(8,128)(2,1)}, u32[]{:S(2)}) copy-start(bf16[384,768]{1,0:T(8,128)(2,1)} %reduce-scatter.2.cloned.1.call-done) | copy-start | bytes 1769476
  216.8 17.7 %all-to-all-start.1 = ((f32[128,1,128]{2,1,0:T(1,128)}), f32[128,1,128]{2,1,0:T(1,128)S(1)}, u32[]{:S(2)}, u32[]{:S(2)}) async-start(f32[128,1,128]{2,1,0:T(1,128)} %broadcast_in_dim.10), calls=%async_computation.2 | async-start | bytes 131072 | tf_op jit(solution)/shard_map/all_to_all | solution.py:34
  225.1 87.5 %all-gather.5.cloned.1.call-start = ((), (), s32[]{:S(2)}) async-start(), calls=%async_computation.6 | async-start | bytes 10027008 | tf_op jit(solution)/shard_map/all_gather | solution.py:77
  242.0 20.4 %all-to-all-start.2 = ((f32[128,1,128]{2,1,0:T(1,128)}), f32[128,1,128]{2,1,0:T(1,128)S(1)}, u32[]{:S(2)}, u32[]{:S(2)}) async-start(f32[128,1,128]{2,1,0:T(1,128)} %broadcast_in_dim.11), calls=%async_computation.3 | async-start | bytes 131072 | tf_op jit(solution)/shard_map/all_to_all | solution.py:34
  312.6 8.2 %copy-start.1 = (bf16[1024,768]{1,0:T(8,128)(2,1)S(1)}, bf16[1024,768]{1,0:T(8,128)(2,1)}, u32[]{:S(2)}) copy-start(bf16[1024,768]{1,0:T(8,128)(2,1)} %param.9) | copy-start | bytes 4718596
Sparse Core Ops, SparseCore 0:
  9.7 70.9 all-gather.2
  130.3 83.0 reduce-scatter.1
  240.1 72.4 all-gather.4

commit v2 on v1

v2 whole, which is shorter than its diff:
```python
import functools
import math

import jax
import jax.numpy as jnp
from jax import lax
from jax.experimental import pallas as pl
from jax.experimental.pallas import tpu as pltpu
from jax.sharding import Mesh
from jax.sharding import PartitionSpec as P

D = 6144
HD = 6144
N_DEV = 128
LANES = 128
SIDE = 4
STRIP = 384
SLAB = SIDE * STRIP
ROWS = 1024
TOK = 128
COLS = 768
MP = 8
WIDTH = 256
EVERY = ("y", "z", "x", "c")
MP_AXES = ("x", "c")


quant_top = 448.0
peak_eps = 1e-06
norm_eps = 1e-06
clip_rms = 0.5
beta_one = 0.9
beta_two = 0.95
bias_one = 1.0 - 0.9**10
bias_two = 1.0 - 0.95**10
adam_eps = 1e-08
rate_value = 0.01
decay_value = 0.1
contract_rows = (((0,), (0,)), ((), ()))


def exchange(rows):
    return lax.all_to_all(rows, EVERY, 0, 0, tiled=True)


def global_max(value):
    return jnp.max(exchange(jnp.broadcast_to(value, (N_DEV, LANES))))


def global_sum(value):
    return jnp.sum(exchange(jnp.broadcast_to(value, (N_DEV, LANES)))[:, 0])


def fetch(array, axis, step):
    size = lax.axis_size(axis)
    return lax.ppermute(array, axis, [((i + step) % size, i) for i in range(size)])


def keep(found, held, top):
    held[...] = found.astype(held.dtype).reshape(held.shape)
    most = jnp.max(jnp.abs(found), axis=0, keepdims=True)
    best = most[:, :LANES]
    for at in range(LANES, COLS, LANES):
        best = jnp.maximum(best, most[:, at : at + LANES])
    top[...] = jnp.maximum(top[...], best)


def product(rows, columns):
    return lax.dot_general(rows, columns, contract_rows, preferred_element_type=jnp.float32)


def own_kernel(places, mine, other, context, held, top, ordered):
    for at in range(MP):
        start = pl.multiple_of(places[at] * TOK, TOK)
        ordered[at * TOK : (at + 1) * TOK, :] = context[pl.ds(start, TOK), :]
    top[...] = jnp.zeros_like(top)
    half = ROWS // 2
    keep(product(mine[...], ordered[:half, :]) + product(other[...], ordered[half:, :]), held, top)


def own_partial(mine, other, context, places):
    return pl.pallas_call(
        own_kernel,
        in_specs=[pl.BlockSpec(memory_space=pltpu.SMEM)] + [pl.BlockSpec(memory_space=pltpu.VMEM)] * 3,
        out_specs=[pl.BlockSpec(memory_space=pltpu.VMEM)] * 2,
        out_shape=[
            jax.ShapeDtypeStruct((SLAB, COLS), jnp.bfloat16),
            jax.ShapeDtypeStruct((N_DEV, LANES), jnp.float32),
        ],
        scratch_shapes=[pltpu.VMEM((ROWS, COLS), jnp.bfloat16)],
        compiler_params=pltpu.CompilerParams(vmem_limit_bytes=60 * 2**20),
        cost_estimate=pl.CostEstimate(
            flops=2 * ROWS * SLAB * COLS,
            bytes_accessed=(ROWS * SLAB + ROWS * COLS + SLAB * COLS) * 2,
            transcendentals=0,
        ),
        name="own_partial",
    )(places, mine, other, context)


def partial_kernel(strips, above, below, upper, lower, held, top):
    which = pl.program_id(0)

    @pl.when(which == 0)
    def _():
        top[...] = jnp.zeros_like(top)

    for index, context in enumerate((above, below)):

        @pl.when(which == index)
        def _(context=context):
            keep(product(strips[...].reshape(ROWS, SLAB), context[...]), held, top)

    @pl.when(which == 2)
    def _():
        rows = strips[...].reshape(2, ROWS // 2, SLAB)
        keep(product(rows[0], upper[...]) + product(rows[1], lower[...]), held, top)


def partial_sums(strips, contexts):
    parts = SIDE - 1
    return pl.pallas_call(
        partial_kernel,
        grid=(parts,),
        in_specs=[pl.BlockSpec((MP, 1, TOK, SLAB), lambda k: (0, k, 0, 0))]
        + [pl.BlockSpec(held.shape, lambda k: (0, 0)) for held in contexts],
        out_specs=[
            pl.BlockSpec((1, SLAB, COLS), lambda k: (k, 0, 0)),
            pl.BlockSpec((N_DEV, LANES), lambda k: (0, 0)),
        ],
        out_shape=[
            jax.ShapeDtypeStruct((parts, SLAB, COLS), jnp.bfloat16),
            jax.ShapeDtypeStruct((N_DEV, LANES), jnp.float32),
        ],
        compiler_params=pltpu.CompilerParams(vmem_limit_bytes=60 * 2**20),
        cost_estimate=pl.CostEstimate(
            flops=2 * parts * ROWS * SLAB * COLS,
            bytes_accessed=parts * (ROWS * SLAB + ROWS * COLS + SLAB * COLS) * 2,
            transcendentals=0,
        ),
        name="partial_sums",
    )(strips, *contexts)


def input_kernel(count, starts, weight, *refs):
    pieces, out, whole, arrived = refs[:count], refs[count], refs[count + 1], refs[count + 2]

    @pl.when(pl.program_id(0) == 0)
    def _():
        copies = []
        for at, piece in enumerate(pieces):
            rows = piece.shape[0]
            start = pl.multiple_of(starts[at], TOK // 2)
            copies.append(pltpu.make_async_copy(piece, whole.at[pl.ds(start, rows), :], arrived.at[at]))
        for copy in copies:
            copy.start()
        for copy in copies:
            copy.wait()

    found = jnp.dot(whole[...], weight[...], preferred_element_type=jnp.float32)
    out[...] = found.astype(out.dtype)


def input_product(pieces, starts, weight):
    count = len(pieces)
    return pl.pallas_call(
        functools.partial(input_kernel, count),
        grid_spec=pltpu.PrefetchScalarGridSpec(
            num_scalar_prefetch=1,
            grid=(COLS // WIDTH,),
            in_specs=[pl.BlockSpec((D, WIDTH), lambda n, at: (0, n))]
            + [pl.BlockSpec(memory_space=pl.ANY)] * count,
            out_specs=pl.BlockSpec((ROWS, WIDTH), lambda n, at: (0, n)),
            scratch_shapes=[pltpu.VMEM((ROWS, D), jnp.bfloat16), pltpu.SemaphoreType.DMA((count,))],
        ),
        out_shape=jax.ShapeDtypeStruct((ROWS, COLS), jnp.bfloat16),
        compiler_params=pltpu.CompilerParams(vmem_limit_bytes=60 * 2**20),
        cost_estimate=pl.CostEstimate(
            flops=2 * ROWS * D * COLS,
            bytes_accessed=(ROWS * D + D * COLS + ROWS * COLS) * 2,
            transcendentals=0,
        ),
        name="input_product",
    )(starts, weight, *pieces)


def neighbours(array, axis):
    return fetch(array, axis, 1), fetch(array, axis, -1)


def opposite(ahead, behind, axis):
    half = ahead.shape[0] // 2
    return fetch(ahead[:half], axis, 1), fetch(behind[half:], axis, -1)


def adam_step(gradient, clip_factor, master, moment_q, second_moment, moment_scale):
    step_grad = clip_factor * gradient
    old_moment = moment_q.astype(jnp.float32) / moment_scale
    moment = beta_one * old_moment + (1.0 - beta_one) * step_grad
    new_second = beta_two * second_moment + (1.0 - beta_two) * step_grad * step_grad
    update = moment / bias_one / (jnp.sqrt(new_second / bias_two) + adam_eps) + decay_value * master
    return moment, new_second, master - rate_value * update


def local(grad_out, context, weight, master, moment_q, second_moment, moment_scale, scale_boost):
    row, column, core = lax.axis_index("y"), lax.axis_index("x"), lax.axis_index("c")
    own = lax.dynamic_slice(grad_out, (0, row * SLAB), (TOK, SLAB))
    blocks = [own] + [fetch(own, "x", step) for step in (1, 3, 2)]
    strips = jnp.stack([grad_out[:, at : at + SLAB] for at in range(0, D, SLAB)])
    strips = lax.all_to_all(strips, "y", 0, 0, tiled=True)
    source, strips, blocks = lax.optimization_barrier((context, strips, blocks))
    strips = jnp.concatenate(
        [lax.dynamic_slice(strips, (lax.rem(row + step, SIDE), 0, 0), (1, TOK, SLAB)) for step in (1, 3, 2)]
    )
    slabs = lax.all_gather(strips, MP_AXES, axis=0, tiled=True).reshape(MP, SIDE - 1, TOK, SLAB)
    above, below = neighbours(source, "y")
    upper, lower = opposite(above, below, "y")
    mine = jnp.concatenate(blocks)
    chips = lax.rem(column + jnp.array((0, 1, 3, 2), jnp.int32), SIDE) * 2
    held_own, top_own = own_partial(mine, fetch(mine, "c", 1), context, jnp.concatenate([chips + core, chips + 1 - core]))
    held, top = partial_sums(slabs, (above, below, upper, lower))
    top = jnp.maximum(top, top_own)
    peak = jnp.max(exchange(top))
    grad_scale = quant_top * scale_boost / (peak + peak_eps)
    total = jnp.zeros((SLAB, COLS), jnp.float32)
    for part in (held_own, held[0], held[1], held[2]):
        total = total + jnp.clip(part.astype(jnp.float32) * grad_scale, -quant_top, quant_top)
    half = TOK // 2
    early, late = grad_out[:half], grad_out[half:]
    total, early, late = lax.optimization_barrier((total.astype(jnp.bfloat16), early, late))
    summed = lax.psum_scatter(total, "z", scatter_dimension=0, tiled=True)
    ahead_early, behind_late = fetch(early, "x", 1), fetch(late, "x", -1)
    summed, ahead_early, behind_late = lax.optimization_barrier((summed, ahead_early, behind_late))
    summed = summed.astype(jnp.float32)
    gradient = summed / grad_scale
    squares = global_sum(jnp.sum(gradient * gradient))
    norm_value = jnp.sqrt(squares + norm_eps)
    clip_factor = clip_rms * math.sqrt(D * HD) / norm_value
    _, _, new_master = adam_step(gradient, clip_factor, master, moment_q, second_moment, moment_scale)
    shard = new_master.astype(jnp.bfloat16)
    (
        shard,
        early,
        late,
        ahead_early,
        behind_late,
        gradient,
        master,
        moment_q,
        second_moment,
    ) = lax.optimization_barrier(
        (shard, early, late, ahead_early, behind_late, gradient, master, moment_q, second_moment)
    )
    new_weight = lax.all_gather(shard, ("y", "z"), axis=0, tiled=True)
    moment, new_second, new_master = adam_step(gradient, clip_factor, master, moment_q, second_moment, moment_scale)
    moment_top = global_max(jnp.max(jnp.abs(moment)))
    new_scale = quant_top / (moment_top + peak_eps)
    new_moment_q = (moment * new_scale).astype(jnp.bfloat16)
    ahead_late, behind_early = fetch(late, "x", 1), fetch(early, "x", -1)
    far_early, far_late = fetch(ahead_early, "x", 1), fetch(behind_late, "x", -1)
    found = (
        (0, 0, grad_out),
        (1, 0, ahead_early),
        (3, half, behind_late),
        (1, half, ahead_late),
        (3, 0, behind_early),
        (2, 0, far_early),
        (2, half, far_late),
    )
    pieces, starts = [], []
    for step, start, piece in found:
        chip = lax.rem(column + step, SIDE) * 2
        pieces += [piece, fetch(piece, "c", 1)]
        starts += [(chip + core) * TOK + start, (chip + 1 - core) * TOK + start]
    input_grad = input_product(pieces, jnp.stack(starts), weight)
    return (input_grad, new_master, new_moment_q, new_second, new_scale, grad_scale, new_weight)


def solution(mesh):
    fine = Mesh(mesh.devices.reshape(SIDE, SIDE, SIDE, 2), EVERY)
    dp, mp = ("y", "z"), MP_AXES
    return jax.shard_map(
        local,
        mesh=fine,
        in_specs=(
            P(dp + mp, None),
            P(dp, mp),
            P(None, mp),
            P(dp, mp),
            P(dp, mp),
            P(dp, mp),
            P(),
            P(),
        ),
        out_specs=(
            P(dp, mp),
            P(dp, mp),
            P(dp, mp),
            P(dp, mp),
            P(),
            P(),
            P(None, mp),
        ),
        check_vma=False,
    )
```

time: 330 us -> 287 us (0.87)
  waiting for transfers between devices: 222 us -> 132 us
  Pallas kernels: 0 us -> 38 us
  matrix products: 33.5 us -> 0 us
  starting transfers between devices: 21.3 us -> 53.8 us
  local copies, waits for them, and re-layouts: 12.1 us -> 20.2 us
    all_gather x2, waiting for transfers between devices: 121 us -> 3.37 us  [the longest x1 3.35 us: local(): lax.all_gather(strips, MP_AXES, axis=0, tiled=True)]
    ppermute x0 -> x21, waiting for transfers between devices: none -> 94 us  [fetch(): lax.ppermute(array, axis, [((i + step) % size, i) for i in range(size)])]
    reduce_scatter x1, waiting for transfers between devices: 83.3 us -> 8.76 us  [local(): summed = lax.psum_scatter(total, 'z', scatter_dimension=0, tiled=True)]
    pallas_call x0 -> x3, Pallas kernels: none -> 38 us  [the longest x1 18.6 us: input_product(): pl.pallas_call(functools.partial(input_kernel, count), grid_spec=pltpu.Pr...]
    dot_general x2 -> x0, matrix products: 33.5 us -> none  [the longest x1 17.7 us: weight_gradient(): lax.dot_general(full_grad, context, contract_rows, preferred_element_type...]
    ppermute x0 -> x21, starting transfers between devices: none -> 27.6 us  [fetch(): lax.ppermute(array, axis, [((i + step) % size, i) for i in range(size)])]
    all_to_all x3 -> x4, waiting for transfers between devices: 17.5 us -> 25.3 us  [the longest x3 25.3 us: exchange(): return lax.all_to_all(rows, EVERY, 0, 0, tiled=True)]
    convert_element_type x3 -> x2, other arithmetic: 16.6 us -> 9.68 us  [the longest x1 5.93 us: local(): total.astype(jnp.bfloat16)]
  transfers between devices with their start and end apart: 6 -> 28, of which waited for: 5 -> 16; matrix products, arithmetic and copies ran while one was open for 6% -> 5% of each run, Pallas kernels for 0% -> 9%
where the time goes in v2:
time: 287 us; the launch traced here: 286 us
  waiting for transfers between devices  132 us (46%)
  starting transfers between devices  53.8 us (19%)
  Pallas kernels  38 us (13%)
  other arithmetic  23.2 us (8%)
  local copies, waits for them, and re-layouts  20.2 us (7%)
  between operations  19.6 us (7%)
    ppermute x21, waiting for transfers between devices, fetch(): lax.ppermute(array, axis, [((i + step) % size, i) for i in range(size)])  94 us
    ppermute x21, starting transfers between devices, fetch(): lax.ppermute(array, axis, [((i + step) % size, i) for i in range(size)])  27.6 us
    all_to_all x3, waiting for transfers between devices, exchange(): return lax.all_to_all(rows, EVERY, 0, 0, tiled=True)  25.3 us
    all_to_all x3, starting transfers between devices, exchange(): return lax.all_to_all(rows, EVERY, 0, 0, tiled=True)  21.1 us
    pallas_call x1, Pallas kernels, input_product(): pl.pallas_call(functools.partial(input_kernel, count), grid_spec=pltpu.Pr...  18.6 us
    pallas_call x1, Pallas kernels, partial_sums(): pl.pallas_call(partial_kernel, grid=(parts,), in_specs=[pl.BlockSpec((MP,...  12.9 us
    unnamed x34, local copies, waits for them, and re-layouts  12.2 us
    reduce_scatter x1, waiting for transfers between devices, local(): summed = lax.psum_scatter(total, 'z', scatter_dimension=0, tiled=True)  8.76 us
  transfers between devices with their start and end apart: 28, of which 16 were waited for; matrix products, arithmetic and copies ran while one was open for 5% of the time, Pallas kernels for 9%

profile of v2, /device:TPU:1, one launch (start us, length us, event | category | flops | bytes accessed | tf_op | source)
XLA Modules:
  0.0 286.4 jit_solution(7383546338068123383)
XLA Ops:
  10.1 5.0 %all-to-all-start = ((bf16[4,128,1536]{2,1,0:T(8,128)(2,1)}), bf16[4,128,1536]{2,1,0:T(8,128)(2,1)S(1)}, u32[]{:S(2)}, u32[]{:S(2)}) async-start(bf16[4,128,1536]{2,1,0:T(8,128)(2,1)} %pad_maximum_fusion), calls=%async_computation | async-start | bytes 3145728 | tf_op jit(solution)/shard_map/all_to_all | solution.py:210
  15.1 2.5 collective-permute-start.1
  19.4 6.5 %collective-permute-done.1 = bf16[128,1536]{1,0:T(8,128)(2,1)S(1)} collective-permute-done((bf16[128,1536]{1,0:T(8,128)(2,1)S(1)}, bf16[128,1536]{1,0:T(8,128)(2,1)S(1)}, u32[]{:S(2)}, u32[]{:S(2)}) %collective-permute-start.1) | collective-permute-done | bytes 393248 | tf_op jit(solution)/shard_map/ppermute | solution.py:56
  25.9 3.3 %collective-permute-done.2 = bf16[128,1536]{1,0:T(8,128)(2,1)S(1)} collective-permute-done((bf16[128,1536]{1,0:T(8,128)(2,1)S(1)}, bf16[128,1536]{1,0:T(8,128)(2,1)S(1)}, u32[]{:S(2)}, u32[]{:S(2)}) %collective-permute-start.2) | collective-permute-done | bytes 393248 | tf_op jit(solution)/shard_map/ppermute | solution.py:56
  29.1 6.6 %collective-permute-done.3 = bf16[128,1536]{1,0:T(8,128)(2,1)S(1)} collective-permute-done((bf16[128,1536]{1,0:T(8,128)(2,1)S(1)}, bf16[128,1536]{1,0:T(8,128)(2,1)S(1)}, u32[]{:S(2)}, u32[]{:S(2)}) %collective-permute-start.3) | collective-permute-done | bytes 393248 | tf_op jit(solution)/shard_map/ppermute | solution.py:56
  37.7 2.5 collective-permute-start.5
  43.2 3.8 %collective-permute-start.4 = (bf16[512,1536]{1,0:T(8,128)(2,1)}, bf16[512,1536]{1,0:T(8,128)(2,1)}, u32[]{:S(2)}, u32[]{:S(2)}) collective-permute-start(bf16[512,1536]{1,0:T(8,128)(2,1)} %constant_dynamic-update-slice_fusion.mine), channel_id=1, source_target_pairs={{1,0},{0,1},{3,2},{2,3},{5,4},{4,5},{7,6},{6,7},{9,8},{8,9},{11,10... | collective-permute-start | bytes 4718600 | tf_op jit(solution)/shard_map/ppermute | solution.py:56
  47.0 23.8 %collective-permute-done.5.above = bf16[1024,768]{1,0:T(8,128)(2,1)S(1)} collective-permute-done((bf16[1024,768]{1,0:T(8,128)(2,1)}, bf16[1024,768]{1,0:T(8,128)(2,1)S(1)}, u32[]{:S(2)}, u32[]{:S(2)}) %collective-permute-start.5) | collective-permute-done | bytes 1572896 | tf_op jit(solution)/shard_map/ppermute | solution.py:56
  70.8 3.4 %collective-permute-start.7 = (bf16[512,768]{1,0:T(8,128)(2,1)S(1)}, bf16[512,768]{1,0:T(8,128)(2,1)S(1)}, u32[]{:S(2)}, u32[]{:S(2)}) collective-permute-start(bf16[512,768]{1,0:T(8,128)(2,1)S(1)} %slice.48), channel_id=1, source_target_pairs={{32,0},{64,32},{96,64},{0,96},{33,1},{65,33},{97,65},{1,97},{34,2}... | collective-permute-start | bytes 2359304 | tf_op jit(solution)/shard_map/ppermute | solution.py:56
  76.3 6.6 %own_partial.1 = (bf16[1536,768]{1,0:T(8,128)(2,1)}, f32[128,128]{1,0:T(8,128)}) custom-call(s32[8]{0:T(128)} %pad_add_fusion.places, bf16[512,1536]{1,0:T(8,128)(2,1)} %constant_dynamic-update-slice_fusion.mine, bf16[512,1536]{1,0:T(8,128)(2,1)} %collective-permute-done.4.other, bf16[1024,768]{1,0:T(8,128)(2,1)} %context.1), custom_call_target="tpu_custom_call" | custom-call | flops 2415919104 | bytes 7077888 | tf_op jit(solution)/shard_map/own_partial/pallas_call | solution.py:82
  82.9 4.0 %collective-permute-done.7.upper = bf16[512,768]{1,0:T(8,128)(2,1)S(1)} collective-permute-done((bf16[512,768]{1,0:T(8,128)(2,1)S(1)}, bf16[512,768]{1,0:T(8,128)(2,1)S(1)}, u32[]{:S(2)}, u32[]{:S(2)}) %collective-permute-start.7) | collective-permute-done | bytes 786464 | tf_op jit(solution)/shard_map/ppermute | solution.py:56
  86.8 4.6 %collective-permute-done.8.lower = bf16[512,768]{1,0:T(8,128)(2,1)} collective-permute-done((bf16[512,768]{1,0:T(8,128)(2,1)S(1)}, bf16[512,768]{1,0:T(8,128)(2,1)}, u32[]{:S(2)}, u32[]{:S(2)}) %collective-permute-start.8) | collective-permute-done | bytes 786464 | tf_op jit(solution)/shard_map/ppermute | solution.py:56
  91.4 3.4 %all-gather.3.cloned.1.call-done = bf16[24,128,1536]{2,1,0:T(8,128)(2,1)} async-done(((bf16[3,128,1536]{2,1,0:T(8,128)(2,1)}), bf16[24,128,1536]{2,1,0:T(8,128)(2,1)}) %all-gather.3.cloned.1.call-update) | async-done | bytes 9437200 | tf_op jit(solution)/shard_map/all_gather | solution.py:215
  94.8 12.9 %partial_sums.1 = (bf16[3,1536,768]{2,1,0:T(8,128)(2,1)}, f32[128,128]{1,0:T(8,128)}) custom-call(bf16[8,3,128,1536]{3,2,1,0:T(8,128)(2,1)} %bitcast.42, bf16[1024,768]{1,0:T(8,128)(2,1)} %copy-done.4, bf16[1024,768]{1,0:T(8,128)(2,1)} %collective-permute-done.6.below, bf16[512,768]{1,0:T(8,128)(2,1)} %copy-done.14, ...), custom_call_target="tpu_custom_call" | custom-call | flops 7247757312 | bytes 21233664 | tf_op jit(solution)/shard_map/partial_sums/pallas_call | solution.py:122
  109.2 9.4 %all-to-all-start.1 = ((f32[128,1,128]{2,1,0:T(1,128)}), f32[128,1,128]{2,1,0:T(1,128)S(1)}, u32[]{:S(2)}, u32[]{:S(2)}) async-start(f32[128,1,128]{2,1,0:T(1,128)} %bitcast.20), calls=%async_computation.1 | async-start | bytes 131072 | tf_op jit(solution)/shard_map/all_to_all | solution.py:43
  120.4 7.7 %all-to-all-done.1 = f32[128,1,128]{2,1,0:T(1,128)S(1)} async-done(((f32[128,1,128]{2,1,0:T(1,128)}), f32[128,1,128]{2,1,0:T(1,128)S(1)}, u32[]{:S(2)}, u32[]{:S(2)}) %all-to-all-start.1) | async-done | bytes 65568 | tf_op jit(solution)/shard_map/all_to_all | solution.py:43
  129.5 5.9 %fusion = bf16[1536,768]{1,0:T(8,128)(2,1)} fusion(bf16[1536,768]{1,0:T(8,128)(2,1)} %get-tuple-element.36, bf16[3,1536,768]{2,1,0:T(8,128)(2,1)} %get-tuple-element.41, f32[]{:T(128)} %div.45), kind=kLoop, calls=%fused_computation.1 | loop fusion | flops 18874368 | bytes 11797504 | tf_op jit(solution)/shard_map/convert_element_type | solution.py:230
  135.8 2.4 collective-permute-start.9
  138.2 17.0 %collective-permute-done.10.refs_4_ = bf16[64,6144]{1,0:T(8,128)(2,1)} collective-permute-done((bf16[64,6144]{1,0:T(8,128)(2,1)}, bf16[64,6144]{1,0:T(8,128)(2,1)}, u32[]{:S(2)}, u32[]{:S(2)}) %collective-permute-start.10) | collective-permute-done | bytes 786464 | tf_op jit(solution)/shard_map/ppermute | solution.py:56
  155.2 8.8 %reduce-scatter.2.cloned.1.call-done = bf16[384,768]{1,0:T(8,128)(2,1)} async-done(((bf16[1536,768]{1,0:T(8,128)(2,1)}), bf16[384,768]{1,0:T(8,128)(2,1)}) %reduce-scatter.2.cloned.1.call-update) | async-done | bytes 589840 | tf_op jit(solution)/shard_map/reduce_scatter | solution.py:231
  164.0 2.0 convert_divide_fusion
  167.3 7.8 %all-to-all-start.2 = ((f32[128,1,128]{2,1,0:T(1,128)}), f32[128,1,128]{2,1,0:T(1,128)S(1)}, u32[]{:S(2)}, u32[]{:S(2)}) async-start(f32[128,1,128]{2,1,0:T(1,128)} %broadcast_in_dim.6), calls=%async_computation.3 | async-start | bytes 131072 | tf_op jit(solution)/shard_map/all_to_all | solution.py:43
  175.8 8.7 %all-to-all-done.2 = f32[128,1,128]{2,1,0:T(1,128)S(1)} async-done(((f32[128,1,128]{2,1,0:T(1,128)}), f32[128,1,128]{2,1,0:T(1,128)S(1)}, u32[]{:S(2)}, u32[]{:S(2)}) %all-to-all-start.2) | async-done | bytes 65568 | tf_op jit(solution)/shard_map/all_to_all | solution.py:43
  185.8 3.7 %subtract_convert_fusion = bf16[384,768]{1,0:T(8,128)(2,1)} fusion(f32[384,768]{1,0:T(8,128)} %param.12, f32[384,768]{1,0:T(8,128)} %param.14, bf16[384,768]{1,0:T(8,128)(2,1)S(1)} %copy-done.1, f32[]{:T(128)S(6)} %div.48, f32[]{:T(128)S(6)} %copy.26, f32[]{:T(128)} %div.45, bf16[384,768]{1,0:T(8,128)(2,1)} %reduce-scatter.2.cloned.1.call-done), kind=kLoop, calls=%fused_computation.19 | loop fusion | flops 6193152 | bytes 4128780 | tf_op jit(solution)/shard_map/convert_element_type | solution.py:240
  192.0 2.1 collective-permute-start.17
  196.2 13.8 %collective-permute-done.13.refs_6_ = bf16[64,6144]{1,0:T(8,128)(2,1)} collective-permute-done((bf16[64,6144]{1,0:T(8,128)(2,1)}, bf16[64,6144]{1,0:T(8,128)(2,1)}, u32[]{:S(2)}, u32[]{:S(2)}) %collective-permute-start.13) | collective-permute-done | bytes 786464 | tf_op jit(solution)/shard_map/ppermute | solution.py:56
  213.7 13.1 %collective-permute-done.17.refs_10_ = bf16[64,6144]{1,0:T(8,128)(2,1)} collective-permute-done((bf16[64,6144]{1,0:T(8,128)(2,1)}, bf16[64,6144]{1,0:T(8,128)(2,1)}, u32[]{:S(2)}, u32[]{:S(2)}) %collective-permute-start.17) | collective-permute-done | bytes 786464 | tf_op jit(solution)/shard_map/ppermute | solution.py:56
  232.0 3.9 %all-to-all-start.3 = ((f32[128,1,128]{2,1,0:T(1,128)}), f32[128,1,128]{2,1,0:T(1,128)S(1)}, u32[]{:S(2)}, u32[]{:S(2)}) async-start(f32[128,1,128]{2,1,0:T(1,128)} %broadcast_in_dim.7), calls=%async_computation.4 | async-start | bytes 131072 | tf_op jit(solution)/shard_map/all_to_all | solution.py:43
  236.6 8.9 %all-to-all-done.3 = f32[128,1,128]{2,1,0:T(1,128)S(1)} async-done(((f32[128,1,128]{2,1,0:T(1,128)}), f32[128,1,128]{2,1,0:T(1,128)S(1)}, u32[]{:S(2)}, u32[]{:S(2)}) %all-to-all-start.3) | async-done | bytes 65568 | tf_op jit(solution)/shard_map/all_to_all | solution.py:43
  246.8 4.2 %multiply_subtract_fusion = (f32[384,768]{1,0:T(8,128)}, f32[384,768]{1,0:T(8,128)}, bf16[384,768]{1,0:T(8,128)(2,1)}) fusion(f32[384,768]{1,0:T(8,128)S(1)} %copy-done.2, f32[384,768]{1,0:T(8,128)S(1)} %get-tuple-element.54, f32[]{:T(128)S(6)} %div.48, f32[]{:T(128)S(6)} %copy.26, bf16[384,768]{1,0:T(8,128)(2,1)S(1)} %copy-done.1, f32[384,768]{1,0:T(8,128)} %param.14, ...), kind=kLoop, calls=%fused_computation.17 | loop fusion | flops 5898240 | bytes 7077900 | tf_op jit(solution)/shard_map/sub | solution.py:202
  251.0 18.6 %input_product.1 = bf16[1024,768]{1,0:T(8,128)(2,1)} custom-call(s32[14]{0:T(128)} %stack.74.starts, bf16[6144,768]{1,0:T(8,128)(2,1)} %weight.1, bf16[128,6144]{1,0:T(8,128)(2,1)} %refs_0_.1, bf16[128,6144]{1,0:T(8,128)(2,1)} %copy-done.13, bf16[64,6144]{1,0:T(8,128)(2,1)} %collective-permute-done.9.refs_2_, ...), custom_call_target="tpu_custom_call" | custom-call | flops 9663676416 | bytes 23592960 | tf_op jit(solution)/shard_map/input_product/pallas_call | solution.py:166
  269.6 8.0 %copy.28 = bf16[6144,768]{1,0:T(8,128)(2,1)} copy(bf16[6144,768]{1,0:T(8,128)(2,1)} %all-gather.5.cloned.1.call-done) | data formatting | bytes 18874368
  (87 shorter events, 32.2 us)
Async XLA Ops:
  10.1 25.6 %all-to-all-start = ((bf16[4,128,1536]{2,1,0:T(8,128)(2,1)}), bf16[4,128,1536]{2,1,0:T(8,128)(2,1)S(1)}, u32[]{:S(2)}, u32[]{:S(2)}) async-start(bf16[4,128,1536]{2,1,0:T(8,128)(2,1)} %pad_maximum_fusion), calls=%async_computation | async-start | bytes 3145728 | tf_op jit(solution)/shard_map/all_to_all | solution.py:210
  15.1 79.7 %all-gather.3.cloned.1.call-start = ((), (), s32[]{:S(2)}) async-start(), calls=%async_computation.5 | async-start | bytes 10616832 | tf_op jit(solution)/shard_map/all_gather | solution.py:215
  15.1 10.7 %collective-permute-start.1 = (bf16[128,1536]{1,0:T(8,128)(2,1)S(1)}, bf16[128,1536]{1,0:T(8,128)(2,1)S(1)}, u32[]{:S(2)}, u32[]{:S(2)}) collective-permute-start(bf16[128,1536]{1,0:T(8,128)(2,1)S(1)} %get-tuple-element.32), channel_id=1, source_target_pairs={{2,0},{4,2},{6,4},{0,6},{3,1},{5,3},{7,5},{1,7},{10,8},{12,10},{14... | collective-permute-start | bytes 1179656 | tf_op jit(solution)/shard_map/ppermute | solution.py:56
  17.6 11.5 %collective-permute-start.2 = (bf16[128,1536]{1,0:T(8,128)(2,1)S(1)}, bf16[128,1536]{1,0:T(8,128)(2,1)S(1)}, u32[]{:S(2)}, u32[]{:S(2)}) collective-permute-start(bf16[128,1536]{1,0:T(8,128)(2,1)S(1)} %get-tuple-element.32), channel_id=1, source_target_pairs={{6,0},{0,2},{2,4},{4,6},{7,1},{1,3},{3,5},{5,7},{14,8},{8,10},{10,... | collective-permute-start | bytes 1179656 | tf_op jit(solution)/shard_map/ppermute | solution.py:56
  17.6 18.1 %collective-permute-start.3 = (bf16[128,1536]{1,0:T(8,128)(2,1)S(1)}, bf16[128,1536]{1,0:T(8,128)(2,1)S(1)}, u32[]{:S(2)}, u32[]{:S(2)}) collective-permute-start(bf16[128,1536]{1,0:T(8,128)(2,1)S(1)} %get-tuple-element.32), channel_id=1, source_target_pairs={{4,0},{6,2},{0,4},{2,6},{5,1},{7,3},{1,5},{3,7},{12,8},{14,10},{8,... | collective-permute-start | bytes 1179656 | tf_op jit(solution)/shard_map/ppermute | solution.py:56
  37.7 33.1 %collective-permute-start.5 = (bf16[1024,768]{1,0:T(8,128)(2,1)}, bf16[1024,768]{1,0:T(8,128)(2,1)S(1)}, u32[]{:S(2)}, u32[]{:S(2)}) collective-permute-start(bf16[1024,768]{1,0:T(8,128)(2,1)} %context.1), channel_id=1, source_target_pairs={{32,0},{64,32},{96,64},{0,96},{33,1},{65,33},{97,65},{1,97},{34,2}... | collective-permute-start | bytes 4718600 | tf_op jit(solution)/shard_map/ppermute | solution.py:56
  40.1 34.1 %collective-permute-start.6 = (bf16[1024,768]{1,0:T(8,128)(2,1)}, bf16[1024,768]{1,0:T(8,128)(2,1)}, u32[]{:S(2)}, u32[]{:S(2)}) collective-permute-start(bf16[1024,768]{1,0:T(8,128)(2,1)} %context.1), channel_id=1, source_target_pairs={{96,0},{0,32},{32,64},{64,96},{97,1},{1,33},{33,65},{65,97},{98,2}... | collective-permute-start | bytes 4718600 | tf_op jit(solution)/shard_map/ppermute | solution.py:56
  43.2 33.1 %collective-permute-start.4 = (bf16[512,1536]{1,0:T(8,128)(2,1)}, bf16[512,1536]{1,0:T(8,128)(2,1)}, u32[]{:S(2)}, u32[]{:S(2)}) collective-permute-start(bf16[512,1536]{1,0:T(8,128)(2,1)} %constant_dynamic-update-slice_fusion.mine), channel_id=1, source_target_pairs={{1,0},{0,1},{3,2},{2,3},{5,4},{4,5},{7,6},{6,7},{9,8},{8,9},{11,10... | collective-permute-start | bytes 4718600 | tf_op jit(solution)/shard_map/ppermute | solution.py:56
  70.8 16.0 %collective-permute-start.7 = (bf16[512,768]{1,0:T(8,128)(2,1)S(1)}, bf16[512,768]{1,0:T(8,128)(2,1)S(1)}, u32[]{:S(2)}, u32[]{:S(2)}) collective-permute-start(bf16[512,768]{1,0:T(8,128)(2,1)S(1)} %slice.48), channel_id=1, source_target_pairs={{32,0},{64,32},{96,64},{0,96},{33,1},{65,33},{97,65},{1,97},{34,2}... | collective-permute-start | bytes 2359304 | tf_op jit(solution)/shard_map/ppermute | solution.py:56
  75.4 16.0 %collective-permute-start.8 = (bf16[512,768]{1,0:T(8,128)(2,1)S(1)}, bf16[512,768]{1,0:T(8,128)(2,1)}, u32[]{:S(2)}, u32[]{:S(2)}) collective-permute-start(bf16[512,768]{1,0:T(8,128)(2,1)S(1)} %slice.49), channel_id=1, source_target_pairs={{96,0},{0,32},{32,64},{64,96},{97,1},{1,33},{33,65},{65,97},{98,2}... | collective-permute-start | bytes 2359304 | tf_op jit(solution)/shard_map/ppermute | solution.py:56
  94.8 23.9 %copy-start = (bf16[128,6144]{1,0:T(8,128)(2,1)S(1)}, bf16[128,6144]{1,0:T(8,128)(2,1)}, u32[]{:S(2)}) copy-start(bf16[128,6144]{1,0:T(8,128)(2,1)} %refs_0_.1) | copy-start | bytes 4718596
  109.2 18.9 %all-to-all-start.1 = ((f32[128,1,128]{2,1,0:T(1,128)}), f32[128,1,128]{2,1,0:T(1,128)S(1)}, u32[]{:S(2)}, u32[]{:S(2)}) async-start(f32[128,1,128]{2,1,0:T(1,128)} %bitcast.20), calls=%async_computation.1 | async-start | bytes 131072 | tf_op jit(solution)/shard_map/all_to_all | solution.py:43
  118.6 45.4 %reduce-scatter.2.cloned.1.call-start = ((), (), s32[]{:S(2)}) async-start(), calls=%async_computation.6 | async-start | bytes 2949120 | tf_op jit(solution)/shard_map/reduce_scatter | solution.py:231
  119.7 16.1 %copy-start.3 = (bf16[64,6144]{1,0:T(8,128)(2,1)}, bf16[64,6144]{1,0:T(8,128)(2,1)S(1)}, u32[]{:S(2)}) copy-start(bf16[64,6144]{1,0:T(8,128)(2,1)S(1)} %get-tuple-element.51) | copy-start | bytes 2359300
  135.4 50.4 %copy-start.1 = (bf16[384,768]{1,0:T(8,128)(2,1)S(1)}, bf16[384,768]{1,0:T(8,128)(2,1)}, u32[]{:S(2)}) copy-start(bf16[384,768]{1,0:T(8,128)(2,1)} %param.13) | copy-start | bytes 1769476
  135.5 19.8 %collective-permute-start.10 = (bf16[64,6144]{1,0:T(8,128)(2,1)}, bf16[64,6144]{1,0:T(8,128)(2,1)}, u32[]{:S(2)}, u32[]{:S(2)}) collective-permute-start(bf16[64,6144]{1,0:T(8,128)(2,1)} %get-tuple-element.50), channel_id=1, source_target_pairs={{6,0},{0,2},{2,4},{4,6},{7,1},{1,3},{3,5},{5,7},{14,8},{8,10},{10,... | collective-permute-start | bytes 2359304 | tf_op jit(solution)/shard_map/ppermute | solution.py:56
  135.8 19.4 %collective-permute-start.9 = (bf16[64,6144]{1,0:T(8,128)(2,1)S(1)}, bf16[64,6144]{1,0:T(8,128)(2,1)}, u32[]{:S(2)}, u32[]{:S(2)}) collective-permute-start(bf16[64,6144]{1,0:T(8,128)(2,1)S(1)} %get-tuple-element.51), channel_id=1, source_target_pairs={{2,0},{4,2},{6,4},{0,6},{3,1},{5,3},{7,5},{1,7},{10,8},{12,10},{14... | collective-permute-start | bytes 2359304 | tf_op jit(solution)/shard_map/ppermute | solution.py:56
  167.3 17.2 %all-to-all-start.2 = ((f32[128,1,128]{2,1,0:T(1,128)}), f32[128,1,128]{2,1,0:T(1,128)S(1)}, u32[]{:S(2)}, u32[]{:S(2)}) async-start(f32[128,1,128]{2,1,0:T(1,128)} %broadcast_in_dim.6), calls=%async_computation.3 | async-start | bytes 131072 | tf_op jit(solution)/shard_map/all_to_all | solution.py:43
  175.1 94.5 %all-gather.5.cloned.1.call-start = ((), (), s32[]{:S(2)}) async-start(), calls=%async_computation.7 | async-start | bytes 10027008 | tf_op jit(solution)/shard_map/all_gather | solution.py:254
  189.6 4.5 %collective-permute-start = (bf16[128,6144]{1,0:T(8,128)(2,1)S(1)}, bf16[128,6144]{1,0:T(8,128)(2,1)S(1)}, u32[]{:S(2)}, u32[]{:S(2)}) collective-permute-start(bf16[128,6144]{1,0:T(8,128)(2,1)S(1)} %copy-done), channel_id=1, source_target_pairs={{1,0},{0,1},{3,2},{2,3},{5,4},{4,5},{7,6},{6,7},{9,8},{8,9},{11,10... | collective-permute-start | bytes 4718600 | tf_op jit(solution)/shard_map/ppermute | solution.py:56
  190.6 19.4 %collective-permute-start.13 = (bf16[64,6144]{1,0:T(8,128)(2,1)}, bf16[64,6144]{1,0:T(8,128)(2,1)}, u32[]{:S(2)}, u32[]{:S(2)}) collective-permute-start(bf16[64,6144]{1,0:T(8,128)(2,1)} %get-tuple-element.50), channel_id=1, source_target_pairs={{2,0},{4,2},{6,4},{0,6},{3,1},{5,3},{7,5},{1,7},{10,8},{12,10},{14... | collective-permute-start | bytes 2359304 | tf_op jit(solution)/shard_map/ppermute | solution.py:56
  191.5 20.3 %collective-permute-start.15 = (bf16[64,6144]{1,0:T(8,128)(2,1)}, bf16[64,6144]{1,0:T(8,128)(2,1)}, u32[]{:S(2)}, u32[]{:S(2)}) collective-permute-start(bf16[64,6144]{1,0:T(8,128)(2,1)} %copy-done.3), channel_id=1, source_target_pairs={{6,0},{0,2},{2,4},{4,6},{7,1},{1,3},{3,5},{5,7},{14,8},{8,10},{10,... | collective-permute-start | bytes 2359304 | tf_op jit(solution)/shard_map/ppermute | solution.py:56
  192.0 34.8 %collective-permute-start.17 = (bf16[64,6144]{1,0:T(8,128)(2,1)}, bf16[64,6144]{1,0:T(8,128)(2,1)}, u32[]{:S(2)}, u32[]{:S(2)}) collective-permute-start(bf16[64,6144]{1,0:T(8,128)(2,1)} %collective-permute-done.9.refs_2_), channel_id=1, source_target_pairs={{2,0},{4,2},{6,4},{0,6},{3,1},{5,3},{7,5},{1,7},{10,8},{12,10},{14... | collective-permute-start | bytes 2359304 | tf_op jit(solution)/shard_map/ppermute | solution.py:56
  194.2 34.5 %collective-permute-start.19 = (bf16[64,6144]{1,0:T(8,128)(2,1)}, bf16[64,6144]{1,0:T(8,128)(2,1)}, u32[]{:S(2)}, u32[]{:S(2)}) collective-permute-start(bf16[64,6144]{1,0:T(8,128)(2,1)} %collective-permute-done.10.refs_4_), channel_id=1, source_target_pairs={{6,0},{0,2},{2,4},{4,6},{7,1},{1,3},{3,5},{5,7},{14,8},{8,10},{10,... | collective-permute-start | bytes 2359304 | tf_op jit(solution)/shard_map/ppermute | solution.py:56
  195.3 51.4 %copy-start.2 = (f32[384,768]{1,0:T(8,128)S(1)}, f32[384,768]{1,0:T(8,128)}, u32[]{:S(2)}) copy-start(f32[384,768]{1,0:T(8,128)} %param.12) | copy-start | bytes 3538948
  195.3 34.5 %collective-permute-start.11 = (bf16[64,6144]{1,0:T(8,128)(2,1)}, bf16[64,6144]{1,0:T(8,128)(2,1)}, u32[]{:S(2)}, u32[]{:S(2)}) collective-permute-start(bf16[64,6144]{1,0:T(8,128)(2,1)} %collective-permute-done.9.refs_2_), channel_id=1, source_target_pairs={{1,0},{0,1},{3,2},{2,3},{5,4},{4,5},{7,6},{6,7},{9,8},{8,9},{11,10... | collective-permute-start | bytes 2359304 | tf_op jit(solution)/shard_map/ppermute | solution.py:56
  210.0 40.9 %collective-permute-start.12 = (bf16[64,6144]{1,0:T(8,128)(2,1)}, bf16[64,6144]{1,0:T(8,128)(2,1)}, u32[]{:S(2)}, u32[]{:S(2)}) collective-permute-start(bf16[64,6144]{1,0:T(8,128)(2,1)} %collective-permute-done.10.refs_4_), channel_id=1, source_target_pairs={{1,0},{0,1},{3,2},{2,3},{5,4},{4,5},{7,6},{6,7},{9,8},{8,9},{11,10... | collective-permute-start | bytes 2359304 | tf_op jit(solution)/shard_map/ppermute | solution.py:56
  211.8 39.2 %collective-permute-start.14 = (bf16[64,6144]{1,0:T(8,128)(2,1)}, bf16[64,6144]{1,0:T(8,128)(2,1)}, u32[]{:S(2)}, u32[]{:S(2)}) collective-permute-start(bf16[64,6144]{1,0:T(8,128)(2,1)} %collective-permute-done.13.refs_6_), channel_id=1, source_target_pairs={{1,0},{0,1},{3,2},{2,3},{5,4},{4,5},{7,6},{6,7},{9,8},{8,9},{11,10... | collective-permute-start | bytes 2359304 | tf_op jit(solution)/shard_map/ppermute | solution.py:56
  226.8 24.1 %collective-permute-start.16 = (bf16[64,6144]{1,0:T(8,128)(2,1)}, bf16[64,6144]{1,0:T(8,128)(2,1)}, u32[]{:S(2)}, u32[]{:S(2)}) collective-permute-start(bf16[64,6144]{1,0:T(8,128)(2,1)} %collective-permute-done.15.refs_8_), channel_id=1, source_target_pairs={{1,0},{0,1},{3,2},{2,3},{5,4},{4,5},{7,6},{6,7},{9,8},{8,9},{11,10... | collective-permute-start | bytes 2359304 | tf_op jit(solution)/shard_map/ppermute | solution.py:56
  228.6 22.3 %collective-permute-start.18 = (bf16[64,6144]{1,0:T(8,128)(2,1)}, bf16[64,6144]{1,0:T(8,128)(2,1)}, u32[]{:S(2)}, u32[]{:S(2)}) collective-permute-start(bf16[64,6144]{1,0:T(8,128)(2,1)} %collective-permute-done.17.refs_10_), channel_id=1, source_target_pairs={{1,0},{0,1},{3,2},{2,3},{5,4},{4,5},{7,6},{6,7},{9,8},{8,9},{11,10... | collective-permute-start | bytes 2359304 | tf_op jit(solution)/shard_map/ppermute | solution.py:56
  229.8 21.1 %collective-permute-start.20 = (bf16[64,6144]{1,0:T(8,128)(2,1)}, bf16[64,6144]{1,0:T(8,128)(2,1)}, u32[]{:S(2)}, u32[]{:S(2)}) collective-permute-start(bf16[64,6144]{1,0:T(8,128)(2,1)} %collective-permute-done.19.refs_12_), channel_id=1, source_target_pairs={{1,0},{0,1},{3,2},{2,3},{5,4},{4,5},{7,6},{6,7},{9,8},{8,9},{11,10... | collective-permute-start | bytes 2359304 | tf_op jit(solution)/shard_map/ppermute | solution.py:56
  232.0 13.5 %all-to-all-start.3 = ((f32[128,1,128]{2,1,0:T(1,128)}), f32[128,1,128]{2,1,0:T(1,128)S(1)}, u32[]{:S(2)}, u32[]{:S(2)}) async-start(f32[128,1,128]{2,1,0:T(1,128)} %broadcast_in_dim.7), calls=%async_computation.4 | async-start | bytes 131072 | tf_op jit(solution)/shard_map/all_to_all | solution.py:43
  (11 other events, 61.1 us)
Sparse Core Ops, SparseCore 0:
  37.8 56.9 all-gather.2
  135.6 28.3 reduce-scatter.1
  189.7 72.7 all-gather.4

commit v3 on v2

v3 whole, which is shorter than its diff:
```python
import functools
import math

import jax
import jax.numpy as jnp
from jax import lax
from jax.experimental import pallas as pl
from jax.experimental.pallas import tpu as pltpu
from jax.sharding import Mesh
from jax.sharding import PartitionSpec as P

D = 6144
HD = 6144
N_DEV = 128
LANES = 128
SIDE = 4
STRIP = 384
SLAB = SIDE * STRIP
ROWS = 1024
TOK = 128
COLS = 768
MP = 8
WIDTH = 256
EVERY = ("y", "z", "x", "c")
MP_AXES = ("x", "c")


quant_top = 448.0
peak_eps = 1e-06
norm_eps = 1e-06
clip_rms = 0.5
beta_one = 0.9
beta_two = 0.95
bias_one = 1.0 - 0.9**10
bias_two = 1.0 - 0.95**10
adam_eps = 1e-08
rate_value = 0.01
decay_value = 0.1
contract_rows = (((0,), (0,)), ((), ()))


def exchange(rows):
    return lax.all_to_all(rows, EVERY, 0, 0, tiled=True)


def fetch(array, axis, step):
    size = lax.axis_size(axis)
    return lax.ppermute(array, axis, [((i + step) % size, i) for i in range(size)])


def keep(found, held, top):
    held[...] = found.astype(held.dtype).reshape(held.shape)
    most = jnp.max(jnp.abs(found), axis=0, keepdims=True)
    best = most[:, :LANES]
    for at in range(LANES, COLS, LANES):
        best = jnp.maximum(best, most[:, at : at + LANES])
    top[...] = jnp.maximum(top[...], best)


def product(rows, columns):
    return lax.dot_general(rows, columns, contract_rows, preferred_element_type=jnp.float32)


def blocks_kernel(count, places, mine, other, *refs):
    contexts, first_top, held, top, ordered = refs[:count], *refs[count:]
    share = MP // count

    @pl.when(pl.program_id(0) == 0)
    def _():
        top[...] = first_top[...]
        for at in range(MP):
            place = places[at]
            for index, context in enumerate(contexts):

                @pl.when(place // share == index)
                def _(at=at, place=place, index=index, context=context):
                    start = pl.multiple_of((place - index * share) * TOK, TOK)
                    ordered[at * TOK : (at + 1) * TOK, :] = context[pl.ds(start, TOK), :]

    half = ROWS // 2
    keep(product(mine[...], ordered[:half, :]) + product(other[...], ordered[half:, :]), held, top)


def blocks_partial(mine, other, contexts, places, top):
    count = len(contexts)
    tile = 512
    strip = pl.BlockSpec((ROWS // 2, tile), lambda i: (0, i))
    return pl.pallas_call(
        functools.partial(blocks_kernel, count),
        grid=(SLAB // tile,),
        in_specs=[pl.BlockSpec(memory_space=pltpu.SMEM), strip, strip]
        + [pl.BlockSpec(held.shape, lambda i: (0, 0)) for held in (*contexts, top)],
        out_specs=[pl.BlockSpec((tile, COLS), lambda i: (i, 0)), pl.BlockSpec((N_DEV, LANES), lambda i: (0, 0))],
        out_shape=[
            jax.ShapeDtypeStruct((SLAB, COLS), jnp.bfloat16),
            jax.ShapeDtypeStruct((N_DEV, LANES), jnp.float32),
        ],
        scratch_shapes=[pltpu.VMEM((ROWS, COLS), jnp.bfloat16)],
        compiler_params=pltpu.CompilerParams(vmem_limit_bytes=60 * 2**20),
        cost_estimate=pl.CostEstimate(
            flops=2 * ROWS * SLAB * COLS,
            bytes_accessed=(ROWS * SLAB + ROWS * COLS + SLAB * COLS) * 2,
            transcendentals=0,
        ),
        name="blocks_partial",
    )(places, mine, other, *contexts, top)


def partial_kernel(strips, above, below, first_top, held, top):
    which = pl.program_id(0)

    @pl.when(which == 0)
    def _():
        top[...] = first_top[...]

    for index, context in enumerate((above, below)):

        @pl.when(which == index)
        def _(context=context):
            keep(product(strips[...].reshape(ROWS, SLAB), context[...]), held, top)


def partial_sums(strips, contexts, top):
    parts = len(contexts)
    return pl.pallas_call(
        partial_kernel,
        grid=(parts,),
        in_specs=[pl.BlockSpec((MP, 1, TOK, SLAB), lambda k: (0, k, 0, 0))]
        + [pl.BlockSpec(held.shape, lambda k: (0, 0)) for held in (*contexts, top)],
        out_specs=[
            pl.BlockSpec((1, SLAB, COLS), lambda k: (k, 0, 0)),
            pl.BlockSpec((N_DEV, LANES), lambda k: (0, 0)),
        ],
        out_shape=[
            jax.ShapeDtypeStruct((parts, SLAB, COLS), jnp.bfloat16),
            jax.ShapeDtypeStruct((N_DEV, LANES), jnp.float32),
        ],
        compiler_params=pltpu.CompilerParams(vmem_limit_bytes=60 * 2**20),
        cost_estimate=pl.CostEstimate(
            flops=2 * parts * ROWS * SLAB * COLS,
            bytes_accessed=parts * (ROWS * SLAB + ROWS * COLS + SLAB * COLS) * 2,
            transcendentals=0,
        ),
        name="partial_sums",
    )(strips, *contexts, top)


def square_kernel(scale, summed, sums):
    gradient = summed[...].astype(jnp.float32) / scale[0]
    found = jnp.sum(gradient * gradient, axis=0, keepdims=True)
    lanes = found[:, :LANES]
    for at in range(LANES, COLS, LANES):
        lanes = lanes + found[:, at : at + LANES]
    sums[...] = jnp.broadcast_to(lanes, sums.shape)


def square_sums(summed, scale):
    return pl.pallas_call(
        square_kernel,
        in_specs=[pl.BlockSpec(memory_space=pltpu.SMEM), pl.BlockSpec(memory_space=pltpu.VMEM)],
        out_shape=jax.ShapeDtypeStruct((N_DEV, LANES), jnp.float32),
        compiler_params=pltpu.CompilerParams(vmem_limit_bytes=60 * 2**20),
        name="square_sums",
    )(scale.reshape(1), summed)


def input_kernel(sizes, starts, weight, *refs):
    count = len(sizes)
    pieces, out, whole, held, arrived, left = refs[:count], *refs[-5:]
    step, steps = pl.program_id(0), COLS // WIDTH

    @pl.when(step == 0)
    def _():
        copies, offset = [], 0
        for at, piece in enumerate(pieces):
            copies.append(pltpu.make_async_copy(piece, whole.at[offset : offset + sizes[at], :], arrived.at[at]))
            offset += sizes[at]
        for copy in copies:
            copy.start()
        for copy in copies:
            copy.wait()

    found = jnp.dot(whole[...], weight[...], preferred_element_type=jnp.float32)
    for index in range(steps):

        @pl.when(step == index)
        def _(index=index):
            held[:, index * WIDTH : (index + 1) * WIDTH] = found.astype(held.dtype)

    @pl.when(step == steps - 1)
    def _():
        copies, offset = [], 0
        for at in range(count):
            start = pl.multiple_of(starts[at], TOK // 2)
            copies.append(
                pltpu.make_async_copy(
                    held.at[offset : offset + sizes[at], :], out.at[pl.ds(start, sizes[at]), :], left.at[at]
                )
            )
            offset += sizes[at]
        for copy in copies:
            copy.start()
        for copy in copies:
            copy.wait()


def input_product(pieces, starts, weight, before=None):
    count = len(pieces)
    sizes = tuple(piece.shape[0] for piece in pieces)
    operands = [jnp.stack(starts), weight, *pieces]
    anywhere = pl.BlockSpec(memory_space=pl.ANY)
    in_specs = [pl.BlockSpec((D, WIDTH), lambda n, at: (0, n))] + [anywhere] * count
    aliases = {}
    if before is not None:
        aliases = {len(operands): 0}
        operands.append(before)
        in_specs.append(anywhere)
    return pl.pallas_call(
        functools.partial(input_kernel, sizes),
        grid_spec=pltpu.PrefetchScalarGridSpec(
            num_scalar_prefetch=1,
            grid=(COLS // WIDTH,),
            in_specs=in_specs,
            out_specs=anywhere,
            scratch_shapes=[
                pltpu.VMEM((sum(sizes), D), jnp.bfloat16),
                pltpu.VMEM((sum(sizes), COLS), jnp.bfloat16),
                pltpu.SemaphoreType.DMA((count,)),
                pltpu.SemaphoreType.DMA((count,)),
            ],
        ),
        out_shape=jax.ShapeDtypeStruct((ROWS, COLS), jnp.bfloat16),
        input_output_aliases=aliases,
        compiler_params=pltpu.CompilerParams(vmem_limit_bytes=60 * 2**20),
        cost_estimate=pl.CostEstimate(
            flops=2 * sum(sizes) * D * COLS,
            bytes_accessed=(sum(sizes) * D + D * COLS + sum(sizes) * COLS) * 2,
            transcendentals=0,
        ),
        name="input_product",
    )(*operands)


def neighbours(array, axis):
    return fetch(array, axis, 1), fetch(array, axis, -1)


def opposite(ahead, behind, axis):
    half = ahead.shape[0] // 2
    return fetch(ahead[:half], axis, 1), fetch(behind[half:], axis, -1)


def adam_step(gradient, clip_factor, master, moment_q, second_moment, moment_scale):
    step_grad = clip_factor * gradient
    old_moment = moment_q.astype(jnp.float32) / moment_scale
    moment = beta_one * old_moment + (1.0 - beta_one) * step_grad
    new_second = beta_two * second_moment + (1.0 - beta_two) * step_grad * step_grad
    update = moment / bias_one / (jnp.sqrt(new_second / bias_two) + adam_eps) + decay_value * master
    return moment, new_second, master - rate_value * update


def local(grad_out, context, weight, master, moment_q, second_moment, moment_scale, scale_boost):
    row, column, core = lax.axis_index("y"), lax.axis_index("x"), lax.axis_index("c")

    def strip(step):
        return lax.dynamic_slice(grad_out, (0, lax.rem(row + step, SIDE) * SLAB), (TOK, SLAB))

    own = strip(0)
    strips = jnp.stack([fetch(strip(3), "y", 1), fetch(strip(1), "y", -1)])
    own_ahead, own_behind = neighbours(own, "x")
    strips, own_ahead, own_behind, own_again, far = lax.optimization_barrier(
        (strips, own_ahead, own_behind, own, strip(2))
    )
    slabs = lax.all_gather(strips, MP_AXES, axis=0, tiled=True).reshape(MP, 2, TOK, SLAB)
    own_far = fetch(own_again, "x", 2)
    far = fetch(far, "y", 2)
    source, own_far, far = lax.optimization_barrier((context, own_far, far))
    above, below = neighbours(source, "y")
    far_ahead, far_behind = neighbours(far, "x")
    upper, lower = opposite(above, below, "y")
    chips = lax.rem(column + jnp.array((0, 1, 3, 2), jnp.int32), SIDE) * 2
    places = jnp.concatenate([chips + core, chips + 1 - core])
    mine = jnp.concatenate([own, own_ahead, own_behind, own_far])
    nothing = jnp.zeros((N_DEV, LANES), jnp.float32)
    held_own, top = blocks_partial(mine, fetch(mine, "c", 1), (context,), places, nothing)
    far, top = lax.optimization_barrier((far, top))
    far_far = fetch(far, "x", 2)
    held, top = partial_sums(slabs, (above, below), top)
    mine = jnp.concatenate([far, far_ahead, far_behind, far_far])
    held_far, top = blocks_partial(mine, fetch(mine, "c", 1), (upper, lower), places, top)
    peak = jnp.max(exchange(top))
    grad_scale = quant_top * scale_boost / (peak + peak_eps)
    limit = quant_top / grad_scale
    total = jnp.zeros((SLAB, COLS), jnp.float32)
    for part in (held_own, held[0], held[1], held_far):
        total = total + jnp.clip(part.astype(jnp.float32), -limit, limit)
    total = (total * grad_scale).astype(jnp.bfloat16)
    half = TOK // 2
    early, late = grad_out[:half], grad_out[half:]
    total, early, late = lax.optimization_barrier((total, early, late))
    summed = lax.psum_scatter(total, "z", scatter_dimension=0, tiled=True)
    ahead_early, behind_late = fetch(early, "x", 1), fetch(late, "x", -1)
    summed, ahead_early, behind_late = lax.optimization_barrier((summed, ahead_early, behind_late))
    squares = jnp.sum(exchange(square_sums(summed, grad_scale)))
    clip_factor = clip_rms * math.sqrt(D * HD) / jnp.sqrt(squares + norm_eps)
    gradient = summed.astype(jnp.float32) / grad_scale
    _, _, new_master = adam_step(gradient, clip_factor, master, moment_q, second_moment, moment_scale)
    shard = new_master.astype(jnp.bfloat16)
    shard, early, late, ahead_early, behind_late, summed = lax.optimization_barrier(
        (shard, early, late, ahead_early, behind_late, summed)
    )
    new_weight = lax.all_gather(shard, ("y", "z"), axis=0, tiled=True)
    gradient = summed.astype(jnp.float32) / grad_scale
    moment, new_second, new_master = adam_step(gradient, clip_factor, master, moment_q, second_moment, moment_scale)
    ahead_late, behind_early = fetch(late, "x", 1), fetch(early, "x", -1)

    def gathered(group, before):
        pieces, starts = [], []
        for step, start, piece in group:
            chip = lax.rem(column + step, SIDE) * 2
            pieces += [piece, fetch(piece, "c", 1)]
            starts += [(chip + core) * TOK + start, (chip + 1 - core) * TOK + start]
        return input_product(pieces, starts, weight, before)

    input_grad = gathered(((0, 0, grad_out), (1, 0, ahead_early), (3, half, behind_late)), None)
    ahead_early, behind_late, input_grad = lax.optimization_barrier((ahead_early, behind_late, input_grad))
    far_early, far_late = fetch(ahead_early, "x", 1), fetch(behind_late, "x", -1)
    moment, far_early, far_late = lax.optimization_barrier((moment, far_early, far_late))
    moment_tops = exchange(jnp.broadcast_to(jnp.max(jnp.abs(moment)), (N_DEV, LANES)))
    others = ((1, half, ahead_late), (3, 0, behind_early), (2, 0, far_early), (2, half, far_late))
    input_grad = gathered(others, input_grad)
    moment_tops, input_grad = lax.optimization_barrier((moment_tops, input_grad))
    new_scale = quant_top / (jnp.max(moment_tops) + peak_eps)
    new_moment_q = (moment * new_scale).astype(jnp.bfloat16)
    return (input_grad, new_master, new_moment_q, new_second, new_scale, grad_scale, new_weight)


def solution(mesh):
    fine = Mesh(mesh.devices.reshape(SIDE, SIDE, SIDE, 2), EVERY)
    dp, mp = ("y", "z"), MP_AXES
    return jax.shard_map(
        local,
        mesh=fine,
        in_specs=(
            P(dp + mp, None),
            P(dp, mp),
            P(None, mp),
            P(dp, mp),
            P(dp, mp),
            P(dp, mp),
            P(),
            P(),
        ),
        out_specs=(
            P(dp, mp),
            P(dp, mp),
            P(dp, mp),
            P(dp, mp),
            P(),
            P(),
            P(None, mp),
        ),
        check_vma=False,
    )
```

time: 287 us -> 277 us (0.965)
  waiting for transfers between devices: 132 us -> 111 us
  Pallas kernels: 38 us -> 49.4 us
  other arithmetic: 23.2 us -> 19.4 us
    ppermute x21 -> x28, waiting for transfers between devices: 94 us -> 78.7 us  [fetch(): lax.ppermute(array, axis, [((i + step) % size, i) for i in range(size)])]
    pallas_call x2 -> x5, Pallas kernels: 25.1 us -> 39.7 us  [the longest x2 24.6 us: input_product(): pl.pallas_call(functools.partial(input_kernel, sizes), grid_spec=pltpu.Pr...]
    all_to_all x3, waiting for transfers between devices: 25.3 us -> 16.4 us  [exchange(): return lax.all_to_all(rows, EVERY, 0, 0, tiled=True)]
    all_gather x1, waiting for transfers between devices: 0.02 us -> 7.05 us  [local(): new_weight = lax.all_gather(shard, ('y', 'z'), axis=0, tiled=True)]
    all_to_all x1 -> x0, starting transfers between devices: 5.01 us -> none  [local(): strips = lax.all_to_all(strips, 'y', 0, 0, tiled=True)]
    all_to_all x3, starting transfers between devices: 21.1 us -> 25 us  [exchange(): return lax.all_to_all(rows, EVERY, 0, 0, tiled=True)]
    ppermute x21 -> x28, starting transfers between devices: 27.6 us -> 31.2 us  [fetch(): lax.ppermute(array, axis, [((i + step) % size, i) for i in range(size)])]
    pallas_call x1, Pallas kernels: 12.9 us -> 9.63 us  [partial_sums(): pl.pallas_call(partial_kernel, grid=(parts,), in_specs=[pl.BlockSpec((MP,...]
  transfers between devices with their start and end apart: 28 -> 34, of which waited for: 16 -> 20; matrix products, arithmetic and copies ran while one was open for 5% -> 7% of each run, Pallas kernels for 9% -> 15%
where the time goes in v3:
time: 277 us; the launch traced here: 276 us
  waiting for transfers between devices  111 us (40%)
  starting transfers between devices  56.4 us (20%)
  Pallas kernels  49.4 us (18%)
  local copies, waits for them, and re-layouts  20.8 us (8%)
  between operations  19.7 us (7%)
  other arithmetic  19.4 us (7%)
    ppermute x28, waiting for transfers between devices, fetch(): lax.ppermute(array, axis, [((i + step) % size, i) for i in range(size)])  78.7 us
    ppermute x28, starting transfers between devices, fetch(): lax.ppermute(array, axis, [((i + step) % size, i) for i in range(size)])  31.2 us
    all_to_all x3, starting transfers between devices, exchange(): return lax.all_to_all(rows, EVERY, 0, 0, tiled=True)  25 us
    pallas_call x2, Pallas kernels, input_product(): pl.pallas_call(functools.partial(input_kernel, sizes), grid_spec=pltpu.Pr...  24.6 us
    all_to_all x3, waiting for transfers between devices, exchange(): return lax.all_to_all(rows, EVERY, 0, 0, tiled=True)  16.4 us
    pallas_call x2, Pallas kernels, blocks_partial(): pl.pallas_call(functools.partial(blocks_kernel, count), grid=(SLAB // til...  13.1 us
    unnamed x24, local copies, waits for them, and re-layouts  12.7 us
    pallas_call x1, Pallas kernels, partial_sums(): pl.pallas_call(partial_kernel, grid=(parts,), in_specs=[pl.BlockSpec((MP,...  9.63 us
  transfers between devices with their start and end apart: 34, of which 20 were waited for; matrix products, arithmetic and copies ran while one was open for 7% of the time, Pallas kernels for 15%

profile of v3, /device:TPU:1, one launch (start us, length us, event | category | flops | bytes accessed | tf_op | source)
XLA Modules:
  0.0 276.4 jit_solution(14563322885567771868)
XLA Ops:
  8.7 2.2 collective-permute-start.1
  15.1 5.9 %collective-permute-done.1 = bf16[128,1536]{1,0:T(8,128)(2,1)S(1)} collective-permute-done((bf16[128,1536]{1,0:T(8,128)(2,1)S(1)}, bf16[128,1536]{1,0:T(8,128)(2,1)S(1)}, u32[]{:S(2)}, u32[]{:S(2)}) %collective-permute-start.1) | collective-permute-done | bytes 393248 | tf_op jit(solution)/shard_map/ppermute | solution.py:48
  23.3 2.2 collective-permute-start.4
  27.0 6.5 %collective-permute-done.4 = bf16[128,1536]{1,0:T(8,128)(2,1)S(1)} collective-permute-done((bf16[128,1536]{1,0:T(8,128)(2,1)S(1)}, bf16[128,1536]{1,0:T(8,128)(2,1)S(1)}, u32[]{:S(2)}, u32[]{:S(2)}) %collective-permute-start.4) | collective-permute-done | bytes 393248 | tf_op jit(solution)/shard_map/ppermute | solution.py:48
  35.1 3.6 %collective-permute-start.6 = (bf16[512,1536]{1,0:T(8,128)(2,1)S(1)}, bf16[512,1536]{1,0:T(8,128)(2,1)}, u32[]{:S(2)}, u32[]{:S(2)}) collective-permute-start(bf16[512,1536]{1,0:T(8,128)(2,1)S(1)} %pad_maximum_fusion.mine), channel_id=1, source_target_pairs={{1,0},{0,1},{3,2},{2,3},{5,4},{4,5},{7,6},{6,7},{9,8},{8,9},{11,10... | collective-permute-start | bytes 4718600 | tf_op jit(solution)/shard_map/ppermute | solution.py:48
  42.2 2.4 collective-permute-start.11
  45.3 6.6 %blocks_partial.2 = (bf16[1536,768]{1,0:T(8,128)(2,1)}, f32[128,128]{1,0:T(8,128)}) custom-call(s32[8]{0:T(128)} %pad_add_fusion.places, bf16[512,1536]{1,0:T(8,128)(2,1)} %copy-done.3, bf16[512,1536]{1,0:T(8,128)(2,1)} %collective-permute-done.6.other, bf16[1024,768]{1,0:T(8,128)(2,1)} %refs_0_.2, f32[128,128]{1,0:T(8,128)} %broadcast_in_dim.6.refs_1_), custom_call_target="tpu_custom_call" | custom-call | flops 2415919104 | bytes 7077888 | tf_op jit(solution)/shard_map/blocks_partial/pallas_call | solution.py:88
  52.7 6.8 %collective-permute-done.7 = bf16[128,1536]{1,0:T(8,128)(2,1)} collective-permute-done((bf16[128,1536]{1,0:T(8,128)(2,1)S(1)}, bf16[128,1536]{1,0:T(8,128)(2,1)}, u32[]{:S(2)}, u32[]{:S(2)}) %collective-permute-start.7) | collective-permute-done | bytes 393248 | tf_op jit(solution)/shard_map/ppermute | solution.py:48
  62.0 14.3 %collective-permute-done.9 = bf16[128,1536]{1,0:T(8,128)(2,1)S(1)} collective-permute-done((bf16[128,1536]{1,0:T(8,128)(2,1)S(1)}, bf16[128,1536]{1,0:T(8,128)(2,1)S(1)}, u32[]{:S(2)}, u32[]{:S(2)}) %collective-permute-start.9) | collective-permute-done | bytes 393248 | tf_op jit(solution)/shard_map/ppermute | solution.py:48
  80.4 2.5 collective-permute-start.12
  83.7 9.6 %partial_sums.1 = (bf16[2,1536,768]{2,1,0:T(8,128)(2,1)}, f32[128,128]{1,0:T(8,128)}) custom-call(bf16[8,2,128,1536]{3,2,1,0:T(8,128)(2,1)} %bitcast.41, bf16[1024,768]{1,0:T(8,128)(2,1)} %collective-permute-done.11.above, bf16[1024,768]{1,0:T(8,128)(2,1)} %copy-done.8, f32[128,128]{1,0:T(8,128)} %get-tuple-element.53.first_top), custom_call_target="tpu_custom_call" | custom-call | flops 4831838208 | bytes 14155776 | tf_op jit(solution)/shard_map/partial_sums/pallas_call | solution.py:125
  93.4 4.2 %collective-permute-done.14.refs_1_ = bf16[512,768]{1,0:T(8,128)(2,1)} collective-permute-done((bf16[512,768]{1,0:T(8,128)(2,1)S(1)}, bf16[512,768]{1,0:T(8,128)(2,1)}, u32[]{:S(2)}, u32[]{:S(2)}) %collective-permute-start.14) | collective-permute-done | bytes 786464 | tf_op jit(solution)/shard_map/ppermute | solution.py:48
  98.2 6.5 %blocks_partial.3 = (bf16[1536,768]{1,0:T(8,128)(2,1)}, f32[128,128]{1,0:T(8,128)}) custom-call(s32[8]{0:T(128)} %pad_add_fusion.places, bf16[512,1536]{1,0:T(8,128)(2,1)} %constant_dynamic-update-slice_fusion.mine, bf16[512,1536]{1,0:T(8,128)(2,1)} %collective-permute-done.10.other, bf16[512,768]{1,0:T(8,128)(2,1)} %collective-permute-done.12.refs_0_, ...), custom_call_target="tpu_custom_call" | custom-call | flops 2415919104 | bytes 7077888 | tf_op jit(solution)/shard_map/blocks_partial/pallas_call | solution.py:88
  104.8 12.3 %all-to-all-start = ((f32[128,1,128]{2,1,0:T(1,128)}), f32[128,1,128]{2,1,0:T(1,128)S(1)}, u32[]{:S(2)}, u32[]{:S(2)}) async-start(f32[128,1,128]{2,1,0:T(1,128)} %bitcast.40), calls=%async_computation | async-start | bytes 131072 | tf_op jit(solution)/shard_map/all_to_all | solution.py:43
  118.8 7.7 %all-to-all-done = f32[128,1,128]{2,1,0:T(1,128)S(1)} async-done(((f32[128,1,128]{2,1,0:T(1,128)}), f32[128,1,128]{2,1,0:T(1,128)S(1)}, u32[]{:S(2)}, u32[]{:S(2)}) %all-to-all-start) | async-done | bytes 65568 | tf_op jit(solution)/shard_map/all_to_all | solution.py:43
  128.0 6.0 %fusion.2 = bf16[1536,768]{1,0:T(8,128)(2,1)} fusion(bf16[1536,768]{1,0:T(8,128)(2,1)} %get-tuple-element.58, bf16[1536,768]{1,0:T(8,128)(2,1)} %get-tuple-element.56, f32[]{:T(128)} %div.50, bf16[2,1536,768]{2,1,0:T(8,128)(2,1)} %get-tuple-element.57, f32[]{:T(128)S(6)} %neg.2, f32[]{:T(128)S(6)} %div.51), kind=kLoop, calls=%fused_computation.3 | loop fusion | flops 20054016 | bytes 11798532 | tf_op jit(solution)/shard_map/convert_element_type | solution.py:297
  135.5 16.8 %collective-permute-done.15.refs_2_ = bf16[64,6144]{1,0:T(8,128)(2,1)} collective-permute-done((bf16[64,6144]{1,0:T(8,128)(2,1)S(1)}, bf16[64,6144]{1,0:T(8,128)(2,1)}, u32[]{:S(2)}, u32[]{:S(2)}) %collective-permute-start.15) | collective-permute-done | bytes 786464 | tf_op jit(solution)/shard_map/ppermute | solution.py:48
  152.4 2.5 collective-permute-done.16.refs_4_
  154.9 7.6 %reduce-scatter.2.cloned.1.call-done.summed = bf16[384,768]{1,0:T(8,128)(2,1)} async-done(((bf16[1536,768]{1,0:T(8,128)(2,1)}), bf16[384,768]{1,0:T(8,128)(2,1)}) %reduce-scatter.2.cloned.1.call-update) | async-done | bytes 589840 | tf_op jit(solution)/shard_map/reduce_scatter | solution.py:301
  162.5 2.0 square_sums.1
  164.6 7.8 %all-to-all-start.1 = ((f32[128,1,128]{2,1,0:T(1,128)}), f32[128,1,128]{2,1,0:T(1,128)S(1)}, u32[]{:S(2)}, u32[]{:S(2)}) async-start(f32[128,1,128]{2,1,0:T(1,128)} %bitcast.39), calls=%async_computation.2 | async-start | bytes 131072 | tf_op jit(solution)/shard_map/all_to_all | solution.py:43
  173.1 8.7 %all-to-all-done.1 = f32[128,1,128]{2,1,0:T(1,128)S(1)} async-done(((f32[128,1,128]{2,1,0:T(1,128)}), f32[128,1,128]{2,1,0:T(1,128)S(1)}, u32[]{:S(2)}, u32[]{:S(2)}) %all-to-all-start.1) | async-done | bytes 65568 | tf_op jit(solution)/shard_map/all_to_all | solution.py:43
  183.3 3.4 %subtract_convert_fusion = bf16[384,768]{1,0:T(8,128)(2,1)} fusion(f32[384,768]{1,0:T(8,128)S(1)} %copy-done.2, bf16[384,768]{1,0:T(8,128)(2,1)S(1)} %copy-done.1, f32[384,768]{1,0:T(8,128)} %param.14, bf16[384,768]{1,0:T(8,128)(2,1)} %param.13, f32[]{:T(128)} %div.50, f32[]{:T(128)S(6)} %div.52, f32[]{:T(128)S(6)} %copy.24), kind=kLoop, calls=%fused_computation.20 | loop fusion | flops 6193152 | bytes 4128780 | tf_op jit(solution)/shard_map/convert_element_type | solution.py:308
  190.3 1.8 collective-permute-done.17.refs_1_
  193.3 12.2 %input_product.2.refs_8_ = bf16[1024,768]{1,0:T(8,128)(2,1)} custom-call(s32[6]{0:T(128)} %stack.66.starts, bf16[6144,768]{1,0:T(8,128)(2,1)} %weight.3, bf16[128,6144]{1,0:T(8,128)(2,1)} %refs_0_.3, bf16[128,6144]{1,0:T(8,128)(2,1)} %collective-permute-done.17.refs_1_, bf16[64,6144]{1,0:T(8,128)(2,1)} %collective-permute-done.15.refs_2_, ...), custom_call_target="tpu_custom_call" | custom-call | flops 4831838208 | bytes 16515072 | tf_op jit(solution)/shard_map/input_product/pallas_call | solution.py:218
  207.0 3.9 %multiply_subtract_fusion = (f32[384,768]{1,0:T(8,128)}, f32[384,768]{1,0:T(8,128)}, f32[384,768]{1,0:T(8,128)S(1)}) fusion(f32[384,768]{1,0:T(8,128)S(1)} %copy-done.2, f32[]{:T(128)} %div.50, bf16[384,768]{1,0:T(8,128)(2,1)S(1)} %copy-done.1, f32[]{:T(128)S(6)} %div.52, f32[384,768]{1,0:T(8,128)} %param.14, f32[]{:T(128)S(6)} %copy.24, ...), kind=kLoop, calls=%fused_computation.16 | loop fusion | flops 5898240 | bytes 7077900 | tf_op jit(solution)/shard_map/sub | solution.py:259
  212.0 12.9 %collective-permute-done.20.refs_4_ = bf16[64,6144]{1,0:T(8,128)(2,1)} collective-permute-done((bf16[64,6144]{1,0:T(8,128)(2,1)}, bf16[64,6144]{1,0:T(8,128)(2,1)}, u32[]{:S(2)}, u32[]{:S(2)}) %collective-permute-start.20) | collective-permute-done | bytes 786464 | tf_op jit(solution)/shard_map/ppermute | solution.py:48
  224.8 1.8 collective-permute-done.21.refs_6_
  230.8 4.9 %all-to-all-start.2 = ((f32[128,1,128]{2,1,0:T(1,128)}), f32[128,1,128]{2,1,0:T(1,128)}, u32[]{:S(2)}, u32[]{:S(2)}) async-start(f32[128,1,128]{2,1,0:T(1,128)} %broadcast_in_dim.7), calls=%async_computation.3 | async-start | bytes 131072 | tf_op jit(solution)/shard_map/all_to_all | solution.py:43
  237.1 12.3 %input_product.3 = bf16[1024,768]{1,0:T(8,128)(2,1)} custom-call(s32[8]{0:T(128)} %stack.75.starts, bf16[6144,768]{1,0:T(8,128)(2,1)} %weight.3, bf16[64,6144]{1,0:T(8,128)(2,1)} %collective-permute-done.22.refs_0_, bf16[64,6144]{1,0:T(8,128)(2,1)} %copy-done.4, bf16[64,6144]{1,0:T(8,128)(2,1)} %collective-permute-done.24.refs_2_, ...), custom_call_target="tpu_custom_call", output_to_operand_aliasing={{}: (10, {})} | custom-call | flops 4831838208 | bytes 16515072 | tf_op jit(solution)/shard_map/input_product/pallas_call | solution.py:218
  252.5 7.0 %all-gather.5.cloned.1.call-done = bf16[6144,768]{1,0:T(8,128)(2,1)} async-done(((bf16[384,768]{1,0:T(8,128)(2,1)}), bf16[6144,768]{1,0:T(8,128)(2,1)}) %all-gather.5.cloned.1.call-update) | async-done | bytes 9437200 | tf_op jit(solution)/shard_map/all_gather | solution.py:312
  259.6 8.0 %copy.26 = bf16[6144,768]{1,0:T(8,128)(2,1)} copy(bf16[6144,768]{1,0:T(8,128)(2,1)} %all-gather.5.cloned.1.call-done) | data formatting | bytes 18874368
  (91 shorter events, 43.4 us)
Async XLA Ops:
  7.2 76.6 %all-gather.3.cloned.1.call-start = ((), (), s32[]{:S(2)}) async-start(), calls=%async_computation.4 | async-start | bytes 7077888 | tf_op jit(solution)/shard_map/all_gather | solution.py:274
  8.7 12.3 %collective-permute-start.1 = (bf16[128,1536]{1,0:T(8,128)(2,1)S(1)}, bf16[128,1536]{1,0:T(8,128)(2,1)S(1)}, u32[]{:S(2)}, u32[]{:S(2)}) collective-permute-start(bf16[128,1536]{1,0:T(8,128)(2,1)S(1)} %get-tuple-element.88), channel_id=1, source_target_pairs={{96,0},{0,32},{32,64},{64,96},{97,1},{1,33},{33,65},{65,97},{98,2}... | collective-permute-start | bytes 1179656 | tf_op jit(solution)/shard_map/ppermute | solution.py:48
  10.9 10.1 %collective-permute-start = (bf16[128,1536]{1,0:T(8,128)(2,1)S(1)}, bf16[128,1536]{1,0:T(8,128)(2,1)S(1)}, u32[]{:S(2)}, u32[]{:S(2)}) collective-permute-start(bf16[128,1536]{1,0:T(8,128)(2,1)S(1)} %get-tuple-element.89), channel_id=1, source_target_pairs={{32,0},{64,32},{96,64},{0,96},{33,1},{65,33},{97,65},{1,97},{34,2}... | collective-permute-start | bytes 1179656 | tf_op jit(solution)/shard_map/ppermute | solution.py:48
  12.4 10.8 %collective-permute-start.3 = (bf16[128,1536]{1,0:T(8,128)(2,1)S(1)}, bf16[128,1536]{1,0:T(8,128)(2,1)S(1)}, u32[]{:S(2)}, u32[]{:S(2)}) collective-permute-start(bf16[128,1536]{1,0:T(8,128)(2,1)S(1)} %get-tuple-element.43), channel_id=1, source_target_pairs={{6,0},{0,2},{2,4},{4,6},{7,1},{1,3},{3,5},{5,7},{14,8},{8,10},{10,... | collective-permute-start | bytes 1179656 | tf_op jit(solution)/shard_map/ppermute | solution.py:48
  13.6 9.6 %collective-permute-start.2 = (bf16[128,1536]{1,0:T(8,128)(2,1)S(1)}, bf16[128,1536]{1,0:T(8,128)(2,1)S(1)}, u32[]{:S(2)}, u32[]{:S(2)}) collective-permute-start(bf16[128,1536]{1,0:T(8,128)(2,1)S(1)} %get-tuple-element.43), channel_id=1, source_target_pairs={{2,0},{4,2},{6,4},{0,6},{3,1},{5,3},{7,5},{1,7},{10,8},{12,10},{14... | collective-permute-start | bytes 1179656 | tf_op jit(solution)/shard_map/ppermute | solution.py:48
  23.3 10.3 %collective-permute-start.4 = (bf16[128,1536]{1,0:T(8,128)(2,1)S(1)}, bf16[128,1536]{1,0:T(8,128)(2,1)S(1)}, u32[]{:S(2)}, u32[]{:S(2)}) collective-permute-start(bf16[128,1536]{1,0:T(8,128)(2,1)S(1)} %get-tuple-element.43), channel_id=1, source_target_pairs={{4,0},{6,2},{0,4},{2,6},{5,1},{7,3},{1,5},{3,7},{12,8},{14,10},{8,... | collective-permute-start | bytes 1179656 | tf_op jit(solution)/shard_map/ppermute | solution.py:48
  25.4 9.5 %collective-permute-start.5 = (bf16[128,1536]{1,0:T(8,128)(2,1)S(1)}, bf16[128,1536]{1,0:T(8,128)(2,1)S(1)}, u32[]{:S(2)}, u32[]{:S(2)}) collective-permute-start(bf16[128,1536]{1,0:T(8,128)(2,1)S(1)} %get-tuple-element.44), channel_id=1, source_target_pairs={{64,0},{96,32},{0,64},{32,96},{65,1},{97,33},{1,65},{33,97},{66,2}... | collective-permute-start | bytes 1179656 | tf_op jit(solution)/shard_map/ppermute | solution.py:48
  35.1 9.5 %collective-permute-start.6 = (bf16[512,1536]{1,0:T(8,128)(2,1)S(1)}, bf16[512,1536]{1,0:T(8,128)(2,1)}, u32[]{:S(2)}, u32[]{:S(2)}) collective-permute-start(bf16[512,1536]{1,0:T(8,128)(2,1)S(1)} %pad_maximum_fusion.mine), channel_id=1, source_target_pairs={{1,0},{0,1},{3,2},{2,3},{5,4},{4,5},{7,6},{6,7},{9,8},{8,9},{11,10... | collective-permute-start | bytes 4718600 | tf_op jit(solution)/shard_map/ppermute | solution.py:48
  39.3 22.0 %collective-permute-start.8 = (bf16[128,1536]{1,0:T(8,128)(2,1)S(1)}, bf16[128,1536]{1,0:T(8,128)(2,1)S(1)}, u32[]{:S(2)}, u32[]{:S(2)}) collective-permute-start(bf16[128,1536]{1,0:T(8,128)(2,1)S(1)} %collective-permute-done.5), channel_id=1, source_target_pairs={{6,0},{0,2},{2,4},{4,6},{7,1},{1,3},{3,5},{5,7},{14,8},{8,10},{10,... | collective-permute-start | bytes 1179656 | tf_op jit(solution)/shard_map/ppermute | solution.py:48
  40.2 19.3 %collective-permute-start.7 = (bf16[128,1536]{1,0:T(8,128)(2,1)S(1)}, bf16[128,1536]{1,0:T(8,128)(2,1)}, u32[]{:S(2)}, u32[]{:S(2)}) collective-permute-start(bf16[128,1536]{1,0:T(8,128)(2,1)S(1)} %collective-permute-done.5), channel_id=1, source_target_pairs={{2,0},{4,2},{6,4},{0,6},{3,1},{5,3},{7,5},{1,7},{10,8},{12,10},{14... | collective-permute-start | bytes 1179656 | tf_op jit(solution)/shard_map/ppermute | solution.py:48
  42.0 36.7 %collective-permute-start.13 = (bf16[1024,768]{1,0:T(8,128)(2,1)}, bf16[1024,768]{1,0:T(8,128)(2,1)S(1)}, u32[]{:S(2)}, u32[]{:S(2)}) collective-permute-start(bf16[1024,768]{1,0:T(8,128)(2,1)} %refs_0_.2), channel_id=1, source_target_pairs={{96,0},{0,32},{32,64},{64,96},{97,1},{1,33},{33,65},{65,97},{98,2}... | collective-permute-start | bytes 4718600 | tf_op jit(solution)/shard_map/ppermute | solution.py:48
  42.2 36.6 %collective-permute-start.11 = (bf16[1024,768]{1,0:T(8,128)(2,1)}, bf16[1024,768]{1,0:T(8,128)(2,1)}, u32[]{:S(2)}, u32[]{:S(2)}) collective-permute-start(bf16[1024,768]{1,0:T(8,128)(2,1)} %refs_0_.2), channel_id=1, source_target_pairs={{32,0},{64,32},{96,64},{0,96},{33,1},{65,33},{97,65},{1,97},{34,2}... | collective-permute-start | bytes 4718600 | tf_op jit(solution)/shard_map/ppermute | solution.py:48
  51.9 24.4 %collective-permute-start.9 = (bf16[128,1536]{1,0:T(8,128)(2,1)S(1)}, bf16[128,1536]{1,0:T(8,128)(2,1)S(1)}, u32[]{:S(2)}, u32[]{:S(2)}) collective-permute-start(bf16[128,1536]{1,0:T(8,128)(2,1)S(1)} %collective-permute-done.5), channel_id=1, source_target_pairs={{4,0},{6,2},{0,4},{2,6},{5,1},{7,3},{1,5},{3,7},{12,8},{14,10},{8,... | collective-permute-start | bytes 1179656 | tf_op jit(solution)/shard_map/ppermute | solution.py:48
  77.1 21.2 %collective-permute-start.10 = (bf16[512,1536]{1,0:T(8,128)(2,1)}, bf16[512,1536]{1,0:T(8,128)(2,1)}, u32[]{:S(2)}, u32[]{:S(2)}) collective-permute-start(bf16[512,1536]{1,0:T(8,128)(2,1)} %constant_dynamic-update-slice_fusion.mine), channel_id=1, source_target_pairs={{1,0},{0,1},{3,2},{2,3},{5,4},{4,5},{7,6},{6,7},{9,8},{8,9},{11,10... | collective-permute-start | bytes 4718600 | tf_op jit(solution)/shard_map/ppermute | solution.py:48
  78.7 18.9 %collective-permute-start.14 = (bf16[512,768]{1,0:T(8,128)(2,1)S(1)}, bf16[512,768]{1,0:T(8,128)(2,1)}, u32[]{:S(2)}, u32[]{:S(2)}) collective-permute-start(bf16[512,768]{1,0:T(8,128)(2,1)S(1)} %slice.25), channel_id=1, source_target_pairs={{96,0},{0,32},{32,64},{64,96},{97,1},{1,33},{33,65},{65,97},{98,2}... | collective-permute-start | bytes 2359304 | tf_op jit(solution)/shard_map/ppermute | solution.py:48
  80.4 17.8 %collective-permute-start.12 = (bf16[512,768]{1,0:T(8,128)(2,1)S(1)}, bf16[512,768]{1,0:T(8,128)(2,1)}, u32[]{:S(2)}, u32[]{:S(2)}) collective-permute-start(bf16[512,768]{1,0:T(8,128)(2,1)S(1)} %slice.24), channel_id=1, source_target_pairs={{32,0},{64,32},{96,64},{0,96},{33,1},{65,33},{97,65},{1,97},{34,2}... | collective-permute-start | bytes 2359304 | tf_op jit(solution)/shard_map/ppermute | solution.py:48
  104.8 21.7 %all-to-all-start = ((f32[128,1,128]{2,1,0:T(1,128)}), f32[128,1,128]{2,1,0:T(1,128)S(1)}, u32[]{:S(2)}, u32[]{:S(2)}) async-start(f32[128,1,128]{2,1,0:T(1,128)} %bitcast.40), calls=%async_computation | async-start | bytes 131072 | tf_op jit(solution)/shard_map/all_to_all | solution.py:43
  117.1 45.5 %reduce-scatter.2.cloned.1.call-start = ((), (), s32[]{:S(2)}) async-start(), calls=%async_computation.5 | async-start | bytes 2949120 | tf_op jit(solution)/shard_map/reduce_scatter | solution.py:301
  134.0 18.4 %collective-permute-start.15 = (bf16[64,6144]{1,0:T(8,128)(2,1)S(1)}, bf16[64,6144]{1,0:T(8,128)(2,1)}, u32[]{:S(2)}, u32[]{:S(2)}) collective-permute-start(bf16[64,6144]{1,0:T(8,128)(2,1)S(1)} %get-tuple-element.72), channel_id=1, source_target_pairs={{2,0},{4,2},{6,4},{0,6},{3,1},{5,3},{7,5},{1,7},{10,8},{12,10},{14... | collective-permute-start | bytes 2359304 | tf_op jit(solution)/shard_map/ppermute | solution.py:48
  135.2 19.7 %collective-permute-start.16 = (bf16[64,6144]{1,0:T(8,128)(2,1)}, bf16[64,6144]{1,0:T(8,128)(2,1)}, u32[]{:S(2)}, u32[]{:S(2)}) collective-permute-start(bf16[64,6144]{1,0:T(8,128)(2,1)} %get-tuple-element.71), channel_id=1, source_target_pairs={{6,0},{0,2},{2,4},{4,6},{7,1},{1,3},{3,5},{5,7},{14,8},{8,10},{10,... | collective-permute-start | bytes 2359304 | tf_op jit(solution)/shard_map/ppermute | solution.py:48
  164.6 17.2 %all-to-all-start.1 = ((f32[128,1,128]{2,1,0:T(1,128)}), f32[128,1,128]{2,1,0:T(1,128)S(1)}, u32[]{:S(2)}, u32[]{:S(2)}) async-start(f32[128,1,128]{2,1,0:T(1,128)} %bitcast.39), calls=%async_computation.2 | async-start | bytes 131072 | tf_op jit(solution)/shard_map/all_to_all | solution.py:43
  172.4 87.2 %all-gather.5.cloned.1.call-start = ((), (), s32[]{:S(2)}) async-start(), calls=%async_computation.6 | async-start | bytes 10027008 | tf_op jit(solution)/shard_map/all_gather | solution.py:312
  187.7 5.5 %collective-permute-start.19 = (bf16[64,6144]{1,0:T(8,128)(2,1)}, bf16[64,6144]{1,0:T(8,128)(2,1)}, u32[]{:S(2)}, u32[]{:S(2)}) collective-permute-start(bf16[64,6144]{1,0:T(8,128)(2,1)} %collective-permute-done.16.refs_4_), channel_id=1, source_target_pairs={{1,0},{0,1},{3,2},{2,3},{5,4},{4,5},{7,6},{6,7},{9,8},{8,9},{11,10... | collective-permute-start | bytes 2359304 | tf_op jit(solution)/shard_map/ppermute | solution.py:48
  188.8 22.1 %collective-permute-start.22 = (bf16[64,6144]{1,0:T(8,128)(2,1)}, bf16[64,6144]{1,0:T(8,128)(2,1)}, u32[]{:S(2)}, u32[]{:S(2)}) collective-permute-start(bf16[64,6144]{1,0:T(8,128)(2,1)} %get-tuple-element.71), channel_id=1, source_target_pairs={{2,0},{4,2},{6,4},{0,6},{3,1},{5,3},{7,5},{1,7},{10,8},{12,10},{14... | collective-permute-start | bytes 2359304 | tf_op jit(solution)/shard_map/ppermute | solution.py:48
  189.7 22.2 %collective-permute-start.24 = (bf16[64,6144]{1,0:T(8,128)(2,1)}, bf16[64,6144]{1,0:T(8,128)(2,1)}, u32[]{:S(2)}, u32[]{:S(2)}) collective-permute-start(bf16[64,6144]{1,0:T(8,128)(2,1)} %copy-done.7), channel_id=1, source_target_pairs={{6,0},{0,2},{2,4},{4,6},{7,1},{1,3},{3,5},{5,7},{14,8},{8,10},{10,... | collective-permute-start | bytes 2359304 | tf_op jit(solution)/shard_map/ppermute | solution.py:48
  205.5 19.3 %collective-permute-start.20 = (bf16[64,6144]{1,0:T(8,128)(2,1)}, bf16[64,6144]{1,0:T(8,128)(2,1)}, u32[]{:S(2)}, u32[]{:S(2)}) collective-permute-start(bf16[64,6144]{1,0:T(8,128)(2,1)} %collective-permute-done.15.refs_2_), channel_id=1, source_target_pairs={{2,0},{4,2},{6,4},{0,6},{3,1},{5,3},{7,5},{1,7},{10,8},{12,10},{14... | collective-permute-start | bytes 2359304 | tf_op jit(solution)/shard_map/ppermute | solution.py:48
  206.7 20.0 %collective-permute-start.21 = (bf16[64,6144]{1,0:T(8,128)(2,1)}, bf16[64,6144]{1,0:T(8,128)(2,1)}, u32[]{:S(2)}, u32[]{:S(2)}) collective-permute-start(bf16[64,6144]{1,0:T(8,128)(2,1)} %collective-permute-done.16.refs_4_), channel_id=1, source_target_pairs={{6,0},{0,2},{2,4},{4,6},{7,1},{1,3},{3,5},{5,7},{14,8},{8,10},{10,... | collective-permute-start | bytes 2359304 | tf_op jit(solution)/shard_map/ppermute | solution.py:48
  210.9 24.8 %collective-permute-start.23 = (bf16[64,6144]{1,0:T(8,128)(2,1)}, bf16[64,6144]{1,0:T(8,128)(2,1)S(1)}, u32[]{:S(2)}, u32[]{:S(2)}) collective-permute-start(bf16[64,6144]{1,0:T(8,128)(2,1)} %collective-permute-done.22.refs_0_), channel_id=1, source_target_pairs={{1,0},{0,1},{3,2},{2,3},{5,4},{4,5},{7,6},{6,7},{9,8},{8,9},{11,10... | collective-permute-start | bytes 2359304 | tf_op jit(solution)/shard_map/ppermute | solution.py:48
  211.9 23.8 %collective-permute-start.25 = (bf16[64,6144]{1,0:T(8,128)(2,1)}, bf16[64,6144]{1,0:T(8,128)(2,1)S(1)}, u32[]{:S(2)}, u32[]{:S(2)}) collective-permute-start(bf16[64,6144]{1,0:T(8,128)(2,1)} %collective-permute-done.24.refs_2_), channel_id=1, source_target_pairs={{1,0},{0,1},{3,2},{2,3},{5,4},{4,5},{7,6},{6,7},{9,8},{8,9},{11,10... | collective-permute-start | bytes 2359304 | tf_op jit(solution)/shard_map/ppermute | solution.py:48
  226.7 9.1 %collective-permute-start.26 = (bf16[64,6144]{1,0:T(8,128)(2,1)}, bf16[64,6144]{1,0:T(8,128)(2,1)S(1)}, u32[]{:S(2)}, u32[]{:S(2)}) collective-permute-start(bf16[64,6144]{1,0:T(8,128)(2,1)} %collective-permute-done.20.refs_4_), channel_id=1, source_target_pairs={{1,0},{0,1},{3,2},{2,3},{5,4},{4,5},{7,6},{6,7},{9,8},{8,9},{11,10... | collective-permute-start | bytes 2359304 | tf_op jit(solution)/shard_map/ppermute | solution.py:48
  228.2 7.6 %collective-permute-start.27 = (bf16[64,6144]{1,0:T(8,128)(2,1)}, bf16[64,6144]{1,0:T(8,128)(2,1)}, u32[]{:S(2)}, u32[]{:S(2)}) collective-permute-start(bf16[64,6144]{1,0:T(8,128)(2,1)} %collective-permute-done.21.refs_6_), channel_id=1, source_target_pairs={{1,0},{0,1},{3,2},{2,3},{5,4},{4,5},{7,6},{6,7},{9,8},{8,9},{11,10... | collective-permute-start | bytes 2359304 | tf_op jit(solution)/shard_map/ppermute | solution.py:48
  230.8 18.7 %all-to-all-start.2 = ((f32[128,1,128]{2,1,0:T(1,128)}), f32[128,1,128]{2,1,0:T(1,128)}, u32[]{:S(2)}, u32[]{:S(2)}) async-start(f32[128,1,128]{2,1,0:T(1,128)} %broadcast_in_dim.7), calls=%async_computation.3 | async-start | bytes 131072 | tf_op jit(solution)/shard_map/all_to_all | solution.py:43
  (12 other events, 145.4 us)
Sparse Core Ops, SparseCore 0:
  23.4 60.3 all-gather.2
  134.1 28.3 reduce-scatter.1
  186.8 72.7 all-gather.4

commit v4 on v3

--- a/solution.py
+++ b/solution.py
@@ -83,7 +83,7 @@
 
 def blocks_partial(mine, other, contexts, places, top):
     count = len(contexts)
-    tile = 512
+    tile = 768
     strip = pl.BlockSpec((ROWS // 2, tile), lambda i: (0, i))
     return pl.pallas_call(
         functools.partial(blocks_kernel, count),

time: 277 us -> 277 us (level)
  no operation moved by 1% of the time
where the time goes in v4:
time: 277 us; the launch traced here: 276 us
  waiting for transfers between devices  111 us (40%)
  starting transfers between devices  56.4 us (20%)
  Pallas kernels  48.5 us (18%)
  local copies, waits for them, and re-layouts  20.8 us (8%)
  between operations  19.7 us (7%)
  other arithmetic  19.4 us (7%)
    ppermute x28, waiting for transfers between devices, fetch(): lax.ppermute(array, axis, [((i + step) % size, i) for i in range(size)])  79.1 us
    ppermute x28, starting transfers between devices, fetch(): lax.ppermute(array, axis, [((i + step) % size, i) for i in range(size)])  31.3 us
    all_to_all x3, starting transfers between devices, exchange(): return lax.all_to_all(rows, EVERY, 0, 0, tiled=True)  25 us
    pallas_call x2, Pallas kernels, input_product(): pl.pallas_call(functools.partial(input_kernel, sizes), grid_spec=pltpu.Pr...  24.6 us
    all_to_all x3, waiting for transfers between devices, exchange(): return lax.all_to_all(rows, EVERY, 0, 0, tiled=True)  16.4 us
    unnamed x24, local copies, waits for them, and re-layouts  12.7 us
    pallas_call x2, Pallas kernels, blocks_partial(): pl.pallas_call(functools.partial(blocks_kernel, count), grid=(SLAB // til...  12.3 us
    pallas_call x1, Pallas kernels, partial_sums(): pl.pallas_call(partial_kernel, grid=(parts,), in_specs=[pl.BlockSpec((MP,...  9.63 us
  transfers between devices with their start and end apart: 34, of which 20 were waited for; matrix products, arithmetic and copies ran while one was open for 7% of the time, Pallas kernels for 15%

profile of v4, /device:TPU:1, one launch (start us, length us, event | category | flops | bytes accessed | tf_op | source)
XLA Modules:
  0.0 276.0 jit_solution(13133649918123353413)
XLA Ops:
  8.7 2.2 collective-permute-start.1
  15.1 5.9 %collective-permute-done.1 = bf16[128,1536]{1,0:T(8,128)(2,1)S(1)} collective-permute-done((bf16[128,1536]{1,0:T(8,128)(2,1)S(1)}, bf16[128,1536]{1,0:T(8,128)(2,1)S(1)}, u32[]{:S(2)}, u32[]{:S(2)}) %collective-permute-start.1) | collective-permute-done | bytes 393248 | tf_op jit(solution)/shard_map/ppermute | solution.py:48
  23.3 2.2 collective-permute-start.4
  27.0 6.5 %collective-permute-done.4 = bf16[128,1536]{1,0:T(8,128)(2,1)S(1)} collective-permute-done((bf16[128,1536]{1,0:T(8,128)(2,1)S(1)}, bf16[128,1536]{1,0:T(8,128)(2,1)S(1)}, u32[]{:S(2)}, u32[]{:S(2)}) %collective-permute-start.4) | collective-permute-done | bytes 393248 | tf_op jit(solution)/shard_map/ppermute | solution.py:48
  35.1 3.6 %collective-permute-start.6 = (bf16[512,1536]{1,0:T(8,128)(2,1)S(1)}, bf16[512,1536]{1,0:T(8,128)(2,1)}, u32[]{:S(2)}, u32[]{:S(2)}) collective-permute-start(bf16[512,1536]{1,0:T(8,128)(2,1)S(1)} %pad_maximum_fusion.mine), channel_id=1, source_target_pairs={{1,0},{0,1},{3,2},{2,3},{5,4},{4,5},{7,6},{6,7},{9,8},{8,9},{11,10... | collective-permute-start | bytes 4718600 | tf_op jit(solution)/shard_map/ppermute | solution.py:48
  42.2 2.4 collective-permute-start.11
  45.3 6.2 %blocks_partial.2 = (bf16[1536,768]{1,0:T(8,128)(2,1)}, f32[128,128]{1,0:T(8,128)}) custom-call(s32[8]{0:T(128)} %pad_add_fusion.places, bf16[512,1536]{1,0:T(8,128)(2,1)} %copy-done.3, bf16[512,1536]{1,0:T(8,128)(2,1)} %collective-permute-done.6.other, bf16[1024,768]{1,0:T(8,128)(2,1)} %refs_0_.2, f32[128,128]{1,0:T(8,128)} %broadcast_in_dim.6.refs_1_), custom_call_target="tpu_custom_call" | custom-call | flops 2415919104 | bytes 7077888 | tf_op jit(solution)/shard_map/blocks_partial/pallas_call | solution.py:88
  52.2 7.2 %collective-permute-done.7 = bf16[128,1536]{1,0:T(8,128)(2,1)} collective-permute-done((bf16[128,1536]{1,0:T(8,128)(2,1)S(1)}, bf16[128,1536]{1,0:T(8,128)(2,1)}, u32[]{:S(2)}, u32[]{:S(2)}) %collective-permute-start.7) | collective-permute-done | bytes 393248 | tf_op jit(solution)/shard_map/ppermute | solution.py:48
  62.0 14.3 %collective-permute-done.9 = bf16[128,1536]{1,0:T(8,128)(2,1)S(1)} collective-permute-done((bf16[128,1536]{1,0:T(8,128)(2,1)S(1)}, bf16[128,1536]{1,0:T(8,128)(2,1)S(1)}, u32[]{:S(2)}, u32[]{:S(2)}) %collective-permute-start.9) | collective-permute-done | bytes 393248 | tf_op jit(solution)/shard_map/ppermute | solution.py:48
  80.4 2.5 collective-permute-start.12
  83.7 9.6 %partial_sums.1 = (bf16[2,1536,768]{2,1,0:T(8,128)(2,1)}, f32[128,128]{1,0:T(8,128)}) custom-call(bf16[8,2,128,1536]{3,2,1,0:T(8,128)(2,1)} %bitcast.41, bf16[1024,768]{1,0:T(8,128)(2,1)} %collective-permute-done.11.above, bf16[1024,768]{1,0:T(8,128)(2,1)} %copy-done.8, f32[128,128]{1,0:T(8,128)} %get-tuple-element.53.first_top), custom_call_target="tpu_custom_call" | custom-call | flops 4831838208 | bytes 14155776 | tf_op jit(solution)/shard_map/partial_sums/pallas_call | solution.py:125
  93.4 4.2 %collective-permute-done.14.refs_1_ = bf16[512,768]{1,0:T(8,128)(2,1)} collective-permute-done((bf16[512,768]{1,0:T(8,128)(2,1)S(1)}, bf16[512,768]{1,0:T(8,128)(2,1)}, u32[]{:S(2)}, u32[]{:S(2)}) %collective-permute-start.14) | collective-permute-done | bytes 786464 | tf_op jit(solution)/shard_map/ppermute | solution.py:48
  98.2 6.2 %blocks_partial.3 = (bf16[1536,768]{1,0:T(8,128)(2,1)}, f32[128,128]{1,0:T(8,128)}) custom-call(s32[8]{0:T(128)} %pad_add_fusion.places, bf16[512,1536]{1,0:T(8,128)(2,1)} %constant_dynamic-update-slice_fusion.mine, bf16[512,1536]{1,0:T(8,128)(2,1)} %collective-permute-done.10.other, bf16[512,768]{1,0:T(8,128)(2,1)} %collective-permute-done.12.refs_0_, ...), custom_call_target="tpu_custom_call" | custom-call | flops 2415919104 | bytes 7077888 | tf_op jit(solution)/shard_map/blocks_partial/pallas_call | solution.py:88
  104.4 12.3 %all-to-all-start = ((f32[128,1,128]{2,1,0:T(1,128)}), f32[128,1,128]{2,1,0:T(1,128)S(1)}, u32[]{:S(2)}, u32[]{:S(2)}) async-start(f32[128,1,128]{2,1,0:T(1,128)} %bitcast.40), calls=%async_computation | async-start | bytes 131072 | tf_op jit(solution)/shard_map/all_to_all | solution.py:43
  118.4 7.7 %all-to-all-done = f32[128,1,128]{2,1,0:T(1,128)S(1)} async-done(((f32[128,1,128]{2,1,0:T(1,128)}), f32[128,1,128]{2,1,0:T(1,128)S(1)}, u32[]{:S(2)}, u32[]{:S(2)}) %all-to-all-start) | async-done | bytes 65568 | tf_op jit(solution)/shard_map/all_to_all | solution.py:43
  127.6 6.0 %fusion.2 = bf16[1536,768]{1,0:T(8,128)(2,1)} fusion(bf16[1536,768]{1,0:T(8,128)(2,1)} %get-tuple-element.58, bf16[1536,768]{1,0:T(8,128)(2,1)} %get-tuple-element.56, f32[]{:T(128)} %div.50, bf16[2,1536,768]{2,1,0:T(8,128)(2,1)} %get-tuple-element.57, f32[]{:T(128)S(6)} %neg.2, f32[]{:T(128)S(6)} %div.51), kind=kLoop, calls=%fused_computation.3 | loop fusion | flops 20054016 | bytes 11798532 | tf_op jit(solution)/shard_map/convert_element_type | solution.py:297
  135.2 16.8 %collective-permute-done.15.refs_2_ = bf16[64,6144]{1,0:T(8,128)(2,1)} collective-permute-done((bf16[64,6144]{1,0:T(8,128)(2,1)S(1)}, bf16[64,6144]{1,0:T(8,128)(2,1)}, u32[]{:S(2)}, u32[]{:S(2)}) %collective-permute-start.15) | collective-permute-done | bytes 786464 | tf_op jit(solution)/shard_map/ppermute | solution.py:48
  152.0 2.5 collective-permute-done.16.refs_4_
  154.5 7.6 %reduce-scatter.2.cloned.1.call-done.summed = bf16[384,768]{1,0:T(8,128)(2,1)} async-done(((bf16[1536,768]{1,0:T(8,128)(2,1)}), bf16[384,768]{1,0:T(8,128)(2,1)}) %reduce-scatter.2.cloned.1.call-update) | async-done | bytes 589840 | tf_op jit(solution)/shard_map/reduce_scatter | solution.py:301
  162.2 2.0 square_sums.1
  164.2 7.8 %all-to-all-start.1 = ((f32[128,1,128]{2,1,0:T(1,128)}), f32[128,1,128]{2,1,0:T(1,128)S(1)}, u32[]{:S(2)}, u32[]{:S(2)}) async-start(f32[128,1,128]{2,1,0:T(1,128)} %bitcast.39), calls=%async_computation.2 | async-start | bytes 131072 | tf_op jit(solution)/shard_map/all_to_all | solution.py:43
  172.7 8.7 %all-to-all-done.1 = f32[128,1,128]{2,1,0:T(1,128)S(1)} async-done(((f32[128,1,128]{2,1,0:T(1,128)}), f32[128,1,128]{2,1,0:T(1,128)S(1)}, u32[]{:S(2)}, u32[]{:S(2)}) %all-to-all-start.1) | async-done | bytes 65568 | tf_op jit(solution)/shard_map/all_to_all | solution.py:43
  182.9 3.4 %subtract_convert_fusion = bf16[384,768]{1,0:T(8,128)(2,1)} fusion(f32[384,768]{1,0:T(8,128)S(1)} %copy-done.2, bf16[384,768]{1,0:T(8,128)(2,1)S(1)} %copy-done.1, f32[384,768]{1,0:T(8,128)} %param.14, bf16[384,768]{1,0:T(8,128)(2,1)} %param.13, f32[]{:T(128)} %div.50, f32[]{:T(128)S(6)} %div.52, f32[]{:T(128)S(6)} %copy.24), kind=kLoop, calls=%fused_computation.20 | loop fusion | flops 6193152 | bytes 4128780 | tf_op jit(solution)/shard_map/convert_element_type | solution.py:308
  189.9 1.8 collective-permute-done.17.refs_1_
  192.9 12.2 %input_product.2.refs_8_ = bf16[1024,768]{1,0:T(8,128)(2,1)} custom-call(s32[6]{0:T(128)} %stack.66.starts, bf16[6144,768]{1,0:T(8,128)(2,1)} %weight.3, bf16[128,6144]{1,0:T(8,128)(2,1)} %refs_0_.3, bf16[128,6144]{1,0:T(8,128)(2,1)} %collective-permute-done.17.refs_1_, bf16[64,6144]{1,0:T(8,128)(2,1)} %collective-permute-done.15.refs_2_, ...), custom_call_target="tpu_custom_call" | custom-call | flops 4831838208 | bytes 16515072 | tf_op jit(solution)/shard_map/input_product/pallas_call | solution.py:218
  206.7 3.9 %multiply_subtract_fusion = (f32[384,768]{1,0:T(8,128)}, f32[384,768]{1,0:T(8,128)}, f32[384,768]{1,0:T(8,128)S(1)}) fusion(f32[384,768]{1,0:T(8,128)S(1)} %copy-done.2, f32[]{:T(128)} %div.50, bf16[384,768]{1,0:T(8,128)(2,1)S(1)} %copy-done.1, f32[]{:T(128)S(6)} %div.52, f32[384,768]{1,0:T(8,128)} %param.14, f32[]{:T(128)S(6)} %copy.24, ...), kind=kLoop, calls=%fused_computation.16 | loop fusion | flops 5898240 | bytes 7077900 | tf_op jit(solution)/shard_map/sub | solution.py:259
  211.6 12.9 %collective-permute-done.20.refs_4_ = bf16[64,6144]{1,0:T(8,128)(2,1)} collective-permute-done((bf16[64,6144]{1,0:T(8,128)(2,1)}, bf16[64,6144]{1,0:T(8,128)(2,1)}, u32[]{:S(2)}, u32[]{:S(2)}) %collective-permute-start.20) | collective-permute-done | bytes 786464 | tf_op jit(solution)/shard_map/ppermute | solution.py:48
  224.5 1.8 collective-permute-done.21.refs_6_
  230.4 4.9 %all-to-all-start.2 = ((f32[128,1,128]{2,1,0:T(1,128)}), f32[128,1,128]{2,1,0:T(1,128)}, u32[]{:S(2)}, u32[]{:S(2)}) async-start(f32[128,1,128]{2,1,0:T(1,128)} %broadcast_in_dim.7), calls=%async_computation.3 | async-start | bytes 131072 | tf_op jit(solution)/shard_map/all_to_all | solution.py:43
  236.8 12.3 %input_product.3 = bf16[1024,768]{1,0:T(8,128)(2,1)} custom-call(s32[8]{0:T(128)} %stack.75.starts, bf16[6144,768]{1,0:T(8,128)(2,1)} %weight.3, bf16[64,6144]{1,0:T(8,128)(2,1)} %collective-permute-done.22.refs_0_, bf16[64,6144]{1,0:T(8,128)(2,1)} %copy-done.4, bf16[64,6144]{1,0:T(8,128)(2,1)} %collective-permute-done.24.refs_2_, ...), custom_call_target="tpu_custom_call", output_to_operand_aliasing={{}: (10, {})} | custom-call | flops 4831838208 | bytes 16515072 | tf_op jit(solution)/shard_map/input_product/pallas_call | solution.py:218
  252.1 7.0 %all-gather.5.cloned.1.call-done = bf16[6144,768]{1,0:T(8,128)(2,1)} async-done(((bf16[384,768]{1,0:T(8,128)(2,1)}), bf16[6144,768]{1,0:T(8,128)(2,1)}) %all-gather.5.cloned.1.call-update) | async-done | bytes 9437200 | tf_op jit(solution)/shard_map/all_gather | solution.py:312
  259.2 8.0 %copy.26 = bf16[6144,768]{1,0:T(8,128)(2,1)} copy(bf16[6144,768]{1,0:T(8,128)(2,1)} %all-gather.5.cloned.1.call-done) | data formatting | bytes 18874368
  (91 shorter events, 43.5 us)
Async XLA Ops:
  7.2 76.6 %all-gather.3.cloned.1.call-start = ((), (), s32[]{:S(2)}) async-start(), calls=%async_computation.4 | async-start | bytes 7077888 | tf_op jit(solution)/shard_map/all_gather | solution.py:274
  8.7 12.3 %collective-permute-start.1 = (bf16[128,1536]{1,0:T(8,128)(2,1)S(1)}, bf16[128,1536]{1,0:T(8,128)(2,1)S(1)}, u32[]{:S(2)}, u32[]{:S(2)}) collective-permute-start(bf16[128,1536]{1,0:T(8,128)(2,1)S(1)} %get-tuple-element.88), channel_id=1, source_target_pairs={{96,0},{0,32},{32,64},{64,96},{97,1},{1,33},{33,65},{65,97},{98,2}... | collective-permute-start | bytes 1179656 | tf_op jit(solution)/shard_map/ppermute | solution.py:48
  10.9 10.1 %collective-permute-start = (bf16[128,1536]{1,0:T(8,128)(2,1)S(1)}, bf16[128,1536]{1,0:T(8,128)(2,1)S(1)}, u32[]{:S(2)}, u32[]{:S(2)}) collective-permute-start(bf16[128,1536]{1,0:T(8,128)(2,1)S(1)} %get-tuple-element.89), channel_id=1, source_target_pairs={{32,0},{64,32},{96,64},{0,96},{33,1},{65,33},{97,65},{1,97},{34,2}... | collective-permute-start | bytes 1179656 | tf_op jit(solution)/shard_map/ppermute | solution.py:48
  12.4 10.8 %collective-permute-start.3 = (bf16[128,1536]{1,0:T(8,128)(2,1)S(1)}, bf16[128,1536]{1,0:T(8,128)(2,1)S(1)}, u32[]{:S(2)}, u32[]{:S(2)}) collective-permute-start(bf16[128,1536]{1,0:T(8,128)(2,1)S(1)} %get-tuple-element.43), channel_id=1, source_target_pairs={{6,0},{0,2},{2,4},{4,6},{7,1},{1,3},{3,5},{5,7},{14,8},{8,10},{10,... | collective-permute-start | bytes 1179656 | tf_op jit(solution)/shard_map/ppermute | solution.py:48
  13.6 9.6 %collective-permute-start.2 = (bf16[128,1536]{1,0:T(8,128)(2,1)S(1)}, bf16[128,1536]{1,0:T(8,128)(2,1)S(1)}, u32[]{:S(2)}, u32[]{:S(2)}) collective-permute-start(bf16[128,1536]{1,0:T(8,128)(2,1)S(1)} %get-tuple-element.43), channel_id=1, source_target_pairs={{2,0},{4,2},{6,4},{0,6},{3,1},{5,3},{7,5},{1,7},{10,8},{12,10},{14... | collective-permute-start | bytes 1179656 | tf_op jit(solution)/shard_map/ppermute | solution.py:48
  23.3 10.3 %collective-permute-start.4 = (bf16[128,1536]{1,0:T(8,128)(2,1)S(1)}, bf16[128,1536]{1,0:T(8,128)(2,1)S(1)}, u32[]{:S(2)}, u32[]{:S(2)}) collective-permute-start(bf16[128,1536]{1,0:T(8,128)(2,1)S(1)} %get-tuple-element.43), channel_id=1, source_target_pairs={{4,0},{6,2},{0,4},{2,6},{5,1},{7,3},{1,5},{3,7},{12,8},{14,10},{8,... | collective-permute-start | bytes 1179656 | tf_op jit(solution)/shard_map/ppermute | solution.py:48
  25.4 9.5 %collective-permute-start.5 = (bf16[128,1536]{1,0:T(8,128)(2,1)S(1)}, bf16[128,1536]{1,0:T(8,128)(2,1)S(1)}, u32[]{:S(2)}, u32[]{:S(2)}) collective-permute-start(bf16[128,1536]{1,0:T(8,128)(2,1)S(1)} %get-tuple-element.44), channel_id=1, source_target_pairs={{64,0},{96,32},{0,64},{32,96},{65,1},{97,33},{1,65},{33,97},{66,2}... | collective-permute-start | bytes 1179656 | tf_op jit(solution)/shard_map/ppermute | solution.py:48
  35.1 9.5 %collective-permute-start.6 = (bf16[512,1536]{1,0:T(8,128)(2,1)S(1)}, bf16[512,1536]{1,0:T(8,128)(2,1)}, u32[]{:S(2)}, u32[]{:S(2)}) collective-permute-start(bf16[512,1536]{1,0:T(8,128)(2,1)S(1)} %pad_maximum_fusion.mine), channel_id=1, source_target_pairs={{1,0},{0,1},{3,2},{2,3},{5,4},{4,5},{7,6},{6,7},{9,8},{8,9},{11,10... | collective-permute-start | bytes 4718600 | tf_op jit(solution)/shard_map/ppermute | solution.py:48
  39.3 22.0 %collective-permute-start.8 = (bf16[128,1536]{1,0:T(8,128)(2,1)S(1)}, bf16[128,1536]{1,0:T(8,128)(2,1)S(1)}, u32[]{:S(2)}, u32[]{:S(2)}) collective-permute-start(bf16[128,1536]{1,0:T(8,128)(2,1)S(1)} %collective-permute-done.5), channel_id=1, source_target_pairs={{6,0},{0,2},{2,4},{4,6},{7,1},{1,3},{3,5},{5,7},{14,8},{8,10},{10,... | collective-permute-start | bytes 1179656 | tf_op jit(solution)/shard_map/ppermute | solution.py:48
  40.2 19.3 %collective-permute-start.7 = (bf16[128,1536]{1,0:T(8,128)(2,1)S(1)}, bf16[128,1536]{1,0:T(8,128)(2,1)}, u32[]{:S(2)}, u32[]{:S(2)}) collective-permute-start(bf16[128,1536]{1,0:T(8,128)(2,1)S(1)} %collective-permute-done.5), channel_id=1, source_target_pairs={{2,0},{4,2},{6,4},{0,6},{3,1},{5,3},{7,5},{1,7},{10,8},{12,10},{14... | collective-permute-start | bytes 1179656 | tf_op jit(solution)/shard_map/ppermute | solution.py:48
  42.0 36.7 %collective-permute-start.13 = (bf16[1024,768]{1,0:T(8,128)(2,1)}, bf16[1024,768]{1,0:T(8,128)(2,1)S(1)}, u32[]{:S(2)}, u32[]{:S(2)}) collective-permute-start(bf16[1024,768]{1,0:T(8,128)(2,1)} %refs_0_.2), channel_id=1, source_target_pairs={{96,0},{0,32},{32,64},{64,96},{97,1},{1,33},{33,65},{65,97},{98,2}... | collective-permute-start | bytes 4718600 | tf_op jit(solution)/shard_map/ppermute | solution.py:48
  42.2 36.6 %collective-permute-start.11 = (bf16[1024,768]{1,0:T(8,128)(2,1)}, bf16[1024,768]{1,0:T(8,128)(2,1)}, u32[]{:S(2)}, u32[]{:S(2)}) collective-permute-start(bf16[1024,768]{1,0:T(8,128)(2,1)} %refs_0_.2), channel_id=1, source_target_pairs={{32,0},{64,32},{96,64},{0,96},{33,1},{65,33},{97,65},{1,97},{34,2}... | collective-permute-start | bytes 4718600 | tf_op jit(solution)/shard_map/ppermute | solution.py:48
  51.4 24.9 %collective-permute-start.9 = (bf16[128,1536]{1,0:T(8,128)(2,1)S(1)}, bf16[128,1536]{1,0:T(8,128)(2,1)S(1)}, u32[]{:S(2)}, u32[]{:S(2)}) collective-permute-start(bf16[128,1536]{1,0:T(8,128)(2,1)S(1)} %collective-permute-done.5), channel_id=1, source_target_pairs={{4,0},{6,2},{0,4},{2,6},{5,1},{7,3},{1,5},{3,7},{12,8},{14,10},{8,... | collective-permute-start | bytes 1179656 | tf_op jit(solution)/shard_map/ppermute | solution.py:48
  77.1 21.2 %collective-permute-start.10 = (bf16[512,1536]{1,0:T(8,128)(2,1)}, bf16[512,1536]{1,0:T(8,128)(2,1)}, u32[]{:S(2)}, u32[]{:S(2)}) collective-permute-start(bf16[512,1536]{1,0:T(8,128)(2,1)} %constant_dynamic-update-slice_fusion.mine), channel_id=1, source_target_pairs={{1,0},{0,1},{3,2},{2,3},{5,4},{4,5},{7,6},{6,7},{9,8},{8,9},{11,10... | collective-permute-start | bytes 4718600 | tf_op jit(solution)/shard_map/ppermute | solution.py:48
  78.7 18.9 %collective-permute-start.14 = (bf16[512,768]{1,0:T(8,128)(2,1)S(1)}, bf16[512,768]{1,0:T(8,128)(2,1)}, u32[]{:S(2)}, u32[]{:S(2)}) collective-permute-start(bf16[512,768]{1,0:T(8,128)(2,1)S(1)} %slice.25), channel_id=1, source_target_pairs={{96,0},{0,32},{32,64},{64,96},{97,1},{1,33},{33,65},{65,97},{98,2}... | collective-permute-start | bytes 2359304 | tf_op jit(solution)/shard_map/ppermute | solution.py:48
  80.4 17.8 %collective-permute-start.12 = (bf16[512,768]{1,0:T(8,128)(2,1)S(1)}, bf16[512,768]{1,0:T(8,128)(2,1)}, u32[]{:S(2)}, u32[]{:S(2)}) collective-permute-start(bf16[512,768]{1,0:T(8,128)(2,1)S(1)} %slice.24), channel_id=1, source_target_pairs={{32,0},{64,32},{96,64},{0,96},{33,1},{65,33},{97,65},{1,97},{34,2}... | collective-permute-start | bytes 2359304 | tf_op jit(solution)/shard_map/ppermute | solution.py:48
  104.4 21.7 %all-to-all-start = ((f32[128,1,128]{2,1,0:T(1,128)}), f32[128,1,128]{2,1,0:T(1,128)S(1)}, u32[]{:S(2)}, u32[]{:S(2)}) async-start(f32[128,1,128]{2,1,0:T(1,128)} %bitcast.40), calls=%async_computation | async-start | bytes 131072 | tf_op jit(solution)/shard_map/all_to_all | solution.py:43
  116.7 45.5 %reduce-scatter.2.cloned.1.call-start = ((), (), s32[]{:S(2)}) async-start(), calls=%async_computation.5 | async-start | bytes 2949120 | tf_op jit(solution)/shard_map/reduce_scatter | solution.py:301
  133.6 18.4 %collective-permute-start.15 = (bf16[64,6144]{1,0:T(8,128)(2,1)S(1)}, bf16[64,6144]{1,0:T(8,128)(2,1)}, u32[]{:S(2)}, u32[]{:S(2)}) collective-permute-start(bf16[64,6144]{1,0:T(8,128)(2,1)S(1)} %get-tuple-element.72), channel_id=1, source_target_pairs={{2,0},{4,2},{6,4},{0,6},{3,1},{5,3},{7,5},{1,7},{10,8},{12,10},{14... | collective-permute-start | bytes 2359304 | tf_op jit(solution)/shard_map/ppermute | solution.py:48
  134.9 19.7 %collective-permute-start.16 = (bf16[64,6144]{1,0:T(8,128)(2,1)}, bf16[64,6144]{1,0:T(8,128)(2,1)}, u32[]{:S(2)}, u32[]{:S(2)}) collective-permute-start(bf16[64,6144]{1,0:T(8,128)(2,1)} %get-tuple-element.71), channel_id=1, source_target_pairs={{6,0},{0,2},{2,4},{4,6},{7,1},{1,3},{3,5},{5,7},{14,8},{8,10},{10,... | collective-permute-start | bytes 2359304 | tf_op jit(solution)/shard_map/ppermute | solution.py:48
  164.2 17.2 %all-to-all-start.1 = ((f32[128,1,128]{2,1,0:T(1,128)}), f32[128,1,128]{2,1,0:T(1,128)S(1)}, u32[]{:S(2)}, u32[]{:S(2)}) async-start(f32[128,1,128]{2,1,0:T(1,128)} %bitcast.39), calls=%async_computation.2 | async-start | bytes 131072 | tf_op jit(solution)/shard_map/all_to_all | solution.py:43
  172.0 87.2 %all-gather.5.cloned.1.call-start = ((), (), s32[]{:S(2)}) async-start(), calls=%async_computation.6 | async-start | bytes 10027008 | tf_op jit(solution)/shard_map/all_gather | solution.py:312
  187.4 5.5 %collective-permute-start.19 = (bf16[64,6144]{1,0:T(8,128)(2,1)}, bf16[64,6144]{1,0:T(8,128)(2,1)}, u32[]{:S(2)}, u32[]{:S(2)}) collective-permute-start(bf16[64,6144]{1,0:T(8,128)(2,1)} %collective-permute-done.16.refs_4_), channel_id=1, source_target_pairs={{1,0},{0,1},{3,2},{2,3},{5,4},{4,5},{7,6},{6,7},{9,8},{8,9},{11,10... | collective-permute-start | bytes 2359304 | tf_op jit(solution)/shard_map/ppermute | solution.py:48
  188.4 22.1 %collective-permute-start.22 = (bf16[64,6144]{1,0:T(8,128)(2,1)}, bf16[64,6144]{1,0:T(8,128)(2,1)}, u32[]{:S(2)}, u32[]{:S(2)}) collective-permute-start(bf16[64,6144]{1,0:T(8,128)(2,1)} %get-tuple-element.71), channel_id=1, source_target_pairs={{2,0},{4,2},{6,4},{0,6},{3,1},{5,3},{7,5},{1,7},{10,8},{12,10},{14... | collective-permute-start | bytes 2359304 | tf_op jit(solution)/shard_map/ppermute | solution.py:48
  189.4 22.2 %collective-permute-start.24 = (bf16[64,6144]{1,0:T(8,128)(2,1)}, bf16[64,6144]{1,0:T(8,128)(2,1)}, u32[]{:S(2)}, u32[]{:S(2)}) collective-permute-start(bf16[64,6144]{1,0:T(8,128)(2,1)} %copy-done.7), channel_id=1, source_target_pairs={{6,0},{0,2},{2,4},{4,6},{7,1},{1,3},{3,5},{5,7},{14,8},{8,10},{10,... | collective-permute-start | bytes 2359304 | tf_op jit(solution)/shard_map/ppermute | solution.py:48
  205.2 19.3 %collective-permute-start.20 = (bf16[64,6144]{1,0:T(8,128)(2,1)}, bf16[64,6144]{1,0:T(8,128)(2,1)}, u32[]{:S(2)}, u32[]{:S(2)}) collective-permute-start(bf16[64,6144]{1,0:T(8,128)(2,1)} %collective-permute-done.15.refs_2_), channel_id=1, source_target_pairs={{2,0},{4,2},{6,4},{0,6},{3,1},{5,3},{7,5},{1,7},{10,8},{12,10},{14... | collective-permute-start | bytes 2359304 | tf_op jit(solution)/shard_map/ppermute | solution.py:48
  206.4 20.0 %collective-permute-start.21 = (bf16[64,6144]{1,0:T(8,128)(2,1)}, bf16[64,6144]{1,0:T(8,128)(2,1)}, u32[]{:S(2)}, u32[]{:S(2)}) collective-permute-start(bf16[64,6144]{1,0:T(8,128)(2,1)} %collective-permute-done.16.refs_4_), channel_id=1, source_target_pairs={{6,0},{0,2},{2,4},{4,6},{7,1},{1,3},{3,5},{5,7},{14,8},{8,10},{10,... | collective-permute-start | bytes 2359304 | tf_op jit(solution)/shard_map/ppermute | solution.py:48
  210.6 24.8 %collective-permute-start.23 = (bf16[64,6144]{1,0:T(8,128)(2,1)}, bf16[64,6144]{1,0:T(8,128)(2,1)S(1)}, u32[]{:S(2)}, u32[]{:S(2)}) collective-permute-start(bf16[64,6144]{1,0:T(8,128)(2,1)} %collective-permute-done.22.refs_0_), channel_id=1, source_target_pairs={{1,0},{0,1},{3,2},{2,3},{5,4},{4,5},{7,6},{6,7},{9,8},{8,9},{11,10... | collective-permute-start | bytes 2359304 | tf_op jit(solution)/shard_map/ppermute | solution.py:48
  211.5 23.8 %collective-permute-start.25 = (bf16[64,6144]{1,0:T(8,128)(2,1)}, bf16[64,6144]{1,0:T(8,128)(2,1)S(1)}, u32[]{:S(2)}, u32[]{:S(2)}) collective-permute-start(bf16[64,6144]{1,0:T(8,128)(2,1)} %collective-permute-done.24.refs_2_), channel_id=1, source_target_pairs={{1,0},{0,1},{3,2},{2,3},{5,4},{4,5},{7,6},{6,7},{9,8},{8,9},{11,10... | collective-permute-start | bytes 2359304 | tf_op jit(solution)/shard_map/ppermute | solution.py:48
  226.3 9.1 %collective-permute-start.26 = (bf16[64,6144]{1,0:T(8,128)(2,1)}, bf16[64,6144]{1,0:T(8,128)(2,1)S(1)}, u32[]{:S(2)}, u32[]{:S(2)}) collective-permute-start(bf16[64,6144]{1,0:T(8,128)(2,1)} %collective-permute-done.20.refs_4_), channel_id=1, source_target_pairs={{1,0},{0,1},{3,2},{2,3},{5,4},{4,5},{7,6},{6,7},{9,8},{8,9},{11,10... | collective-permute-start | bytes 2359304 | tf_op jit(solution)/shard_map/ppermute | solution.py:48
  227.8 7.6 %collective-permute-start.27 = (bf16[64,6144]{1,0:T(8,128)(2,1)}, bf16[64,6144]{1,0:T(8,128)(2,1)}, u32[]{:S(2)}, u32[]{:S(2)}) collective-permute-start(bf16[64,6144]{1,0:T(8,128)(2,1)} %collective-permute-done.21.refs_6_), channel_id=1, source_target_pairs={{1,0},{0,1},{3,2},{2,3},{5,4},{4,5},{7,6},{6,7},{9,8},{8,9},{11,10... | collective-permute-start | bytes 2359304 | tf_op jit(solution)/shard_map/ppermute | solution.py:48
  230.4 18.7 %all-to-all-start.2 = ((f32[128,1,128]{2,1,0:T(1,128)}), f32[128,1,128]{2,1,0:T(1,128)}, u32[]{:S(2)}, u32[]{:S(2)}) async-start(f32[128,1,128]{2,1,0:T(1,128)} %broadcast_in_dim.7), calls=%async_computation.3 | async-start | bytes 131072 | tf_op jit(solution)/shard_map/all_to_all | solution.py:43
  (12 other events, 145.0 us)
Sparse Core Ops, SparseCore 0:
  23.4 60.3 all-gather.2
  133.7 28.3 reduce-scatter.1
  186.4 72.7 all-gather.4
